TPU v7x, 32 devices: a whole 2x2x4 slice. The times are simulated.
32 devices in a mesh: seq: 4 (over x, core), clip: 8 (over z, y).
Axes of the slice: x: 2, y: 2, z: 4, core: 2. Of those that a mesh axis runs over, the one named last changes fastest.
Arguments:
- x_vis: bfloat16 [24, 157, 768], P('clip'), may hold values from -6 to 6
- vis_pos: int32 [24, 157], P('clip'), may hold values from 0 to 1567, as said below
- w_proj: bfloat16 [768, 384], replicated, may hold values from -0.21875 to 0.21875
- b_proj: float32 [384], replicated, may hold values from -3 to 3
- mask_token: float32 [384], replicated, may hold values from -4 to 4
- ln1_gain: float32 [384], replicated, may hold values from 0.25 to 1.75
- ln1_bias: float32 [384], replicated, may hold values from -2 to 2
- w_qkv: bfloat16 [384, 1152], replicated, may hold values from -0.3125 to 0.3125
- q_bias: float32 [384], replicated, may hold values from -2 to 2
- v_bias: float32 [384], replicated, may hold values from -3 to 3
- w_out: bfloat16 [384, 384], replicated, may hold values from -4 to 4
- b_out: float32 [384], replicated, may hold values from -2 to 2
- ln2_gain: float32 [384], replicated, may hold values from 0.25 to 1.75
- ln2_bias: float32 [384], replicated, may hold values from -2 to 2
- w_fc1: bfloat16 [384, 1536], replicated, may hold values from -0.3125 to 0.3125
- b_fc1: float32 [1536], replicated, may hold values from -3 to 3
- w_fc2: bfloat16 [1536, 384], replicated, may hold values from -0.15625 to 0.15625
- b_fc2: float32 [384], replicated, may hold values from -2 to 2
- cotangent: bfloat16 [24, 1568, 384], P('clip', 'seq'), may hold values from -6 to 6
Outputs:
- output: bfloat16 [24, 1568, 384], P('clip', 'seq')
- grad_x: float32 [24, 157, 768], P('clip')
- grad_w_proj: float32 [768, 384], replicated
- grad_b_proj: float32 [384], replicated
- grad_mask: float32 [384], replicated
- grad_ln1_gain: float32 [384], replicated
- grad_ln1_bias: float32 [384], replicated
- grad_w_qkv: float32 [384, 1152], replicated
- grad_q_bias: float32 [384], replicated
- grad_v_bias: float32 [384], replicated
- grad_w_out: float32 [384, 384], replicated
- grad_b_out: float32 [384], replicated
- grad_ln2_gain: float32 [384], replicated
- grad_ln2_bias: float32 [384], replicated
- grad_w_fc1: float32 [384, 1536], replicated
- grad_b_fc1: float32 [1536], replicated
- grad_w_fc2: float32 [1536, 384], replicated
- grad_b_fc2: float32 [384], replicated
- trust: float32 [4], replicated
- trust_qkv: float32 [1], replicated
Inputs may be any that keep to these rules, and one draw needn't show every extreme that they name: `vis_pos`: each clip's 157 visible positions, in rising order, all different.
All inputs are finite; a program needn't handle non-finite values.
Results may differ from a plain program's by a relative error of at most 0.01.
Values may be sent and summed in bfloat16 or wider, within the bound.
No kernel may reach another device: no remote copies, remote signals or barrier semaphores. Data moves between devices by JAX's collectives and lax.ppermute only.
A program may use at most 256 MiB of HBM per device.

v0:
```python
import functools

import jax
import jax.numpy as jnp
import numpy as np
from jax import lax
from jax.experimental import pallas as pl
from jax.experimental.pallas import tpu as pltpu
from jax.sharding import PartitionSpec as P

D = 384
HEADS = 6
HEAD = 64
PAIRS = 3
PAIR = 128
FF = 1536
DIN = 768
SLOT = 160
LEN = 1568
STEP = 112
BLOCK = 256
BLOCKS = FF // BLOCK
SLOTS = 4
UNROLL_F = True
UNROLL_M = False
UNROLL_B = False
FC_USED = 10392
QKV_USED = 5784
AXES = ("seq", "clip")
VMEM = 60 * 1024 * 1024

bf16 = jnp.bfloat16
f32 = jnp.float32


def dot(left, right):
    return lax.dot_general(
        left, right, (((1,), (0,)), ((), ())), preferred_element_type=f32
    )


def dot_rt(left, right):
    return lax.dot_general(
        left, right, (((1,), (1,)), ((), ())), preferred_element_type=f32
    )


def dot_lt(left, right):
    return lax.dot_general(
        left, right, (((0,), (0,)), ((), ())), preferred_element_type=f32
    )


def split3(value):
    high = value.astype(bf16)
    rest = value - high.astype(f32)
    middle = rest.astype(bf16)
    low = (rest - middle.astype(f32)).astype(bf16)
    return high, middle, low


def sinusoid_table(length, columns):
    positions = np.arange(length, dtype=np.float64)[:, None]
    column = np.arange(columns)
    angles = positions / np.power(10000.0, (2 * (column // 2)) / columns)[None, :]
    return np.where((column % 2)[None, :] == 0, np.sin(angles), np.cos(angles)).astype(np.float32)


def row_loop(total, body, carry, unroll=False):
    full = total // STEP

    def at_step(number, carry):
        return body(pl.ds(pl.multiple_of(number * STEP, STEP), STEP), carry)

    carry = lax.fori_loop(0, full, at_step, carry, unroll=unroll)
    if total % STEP:
        carry = body(pl.ds(full * STEP, total % STEP), carry)
    return carry


def own_lanes(head):
    lane = lax.broadcasted_iota(jnp.int32, (1, PAIR), 1)
    return (lane < HEAD) if head == 0 else (lane >= HEAD)


def column_sums(value):
    return jnp.sum(value, axis=0, keepdims=True)


def square_sum(ref):
    rows, columns = ref.shape
    size = 64

    def add(number, total):
        piece = ref[pl.ds(pl.multiple_of(number * size, size), size), :].astype(f32)
        sums = column_sums(piece * piece)
        for first in range(0, columns, PAIR):
            total = total + sums[:, first : first + PAIR]
        return total

    return lax.fori_loop(0, rows // size, add, jnp.zeros((1, PAIR), f32))


def lane_mean(value):
    return jnp.mean(value, axis=1, keepdims=True)


def forward_kernel(
    start_ref,
    x_ref,
    pos_ref,
    table_ref,
    w_proj_ref,
    b_proj_ref,
    mask_ref,
    gain1_ref,
    bias1_ref,
    w_qkv_ref,
    q_bias_ref,
    v_bias_ref,
    b_out_ref,
    gain2_ref,
    bias2_ref,
    b_fc1_ref,
    b_fc2_ref,
    w_out_hbm,
    w_fc1_hbm,
    w_fc2_hbm,
    cot_hbm,
    gs_ref,
    extra_ref,
    norms_ref,
    out_hbm,
    gmid_hbm,
    kept_hbm,
    sent_hbm,
    p_hbm,
    q_hbm,
    k_hbm,
    v_hbm,
    normed_hbm,
    xhat_hbm,
    rstd_hbm,
    p_s,
    q_s,
    k_s,
    v_s,
    normed_s,
    xhat_s,
    rstd_s,
    emb_s,
    middle_s,
    att_s,
    linv_s,
    attended_s,
    xhat2_s,
    rstd2_s,
    normed2_s,
    gn_s,
    vec_s,
    flat_s,
    out_s,
    w_out_s,
    w_fc1_s,
    w_fc2_s,
    cot_s,
    b_fc1_s,
    save_sems,
    p_sems,
    load_sems,
    end_sems,
    *,
    rows,
    clips,
):
    step = pl.program_id(0)
    half = kept_hbm.shape[0]

    def loads():
        pairs = [
            (w_out_hbm, w_out_s),
            (w_fc1_hbm, w_fc1_s),
            (w_fc2_hbm, w_fc2_s),
            (cot_hbm, cot_s),
        ]
        return [
            pltpu.make_async_copy(source, target, load_sems.at[index])
            for index, (source, target) in enumerate(pairs)
        ]

    def saves(number):
        pairs = [
            (q_s, q_hbm),
            (k_s, k_hbm),
            (v_s, v_hbm),
            (normed_s, normed_hbm),
            (xhat_s, xhat_hbm),
            (rstd_s, rstd_hbm),
        ]
        return [
            pltpu.make_async_copy(source, target.at[number], save_sems.at[index])
            for index, (source, target) in enumerate(pairs)
        ]

    def p_save(number):
        slot = lax.rem(number, SLOTS)
        at = lax.div(number, PAIRS)
        pair = lax.rem(number, PAIRS)
        return pltpu.make_async_copy(
            p_s.at[slot], p_hbm.at[at, pl.ds(2 * pair, 2)], p_sems.at[slot]
        )

    @pl.when(step == 0)
    def _():
        for copy in loads():
            copy.start()

    @pl.when(jnp.logical_and(step > 0, step < clips))
    def _():
        for copy in saves(step - 1):
            copy.wait()
        for number in range(PAIRS - 1):
            p_save(PAIRS * (step - 1) + number).wait()

    @pl.when(jnp.logical_and(step > 1, step < clips))
    def _():
        p_save(PAIRS * (step - 1) - 1).wait()

    @pl.when(step < clips)
    def _():
        projected = dot(x_ref[0], w_proj_ref[...]) + b_proj_ref[...][None, :]
        high, middle, low = split3(projected - mask_ref[...][None, :])
        row = lax.broadcasted_iota(jnp.int32, (LEN, 1), 0)
        onehot = (row == pos_ref[0]).astype(f32).astype(bf16)[:, : x_ref.shape[1]]
        emb_s[...] = (
            (table_ref[...].reshape(LEN, D) + mask_ref[...][None, :])
            + dot(onehot, low)
            + dot(onehot, middle)
        ) + dot(onehot, high)
        for number in range(LEN // STEP):
            at = slice(number * STEP, (number + 1) * STEP)
            value = emb_s[at, :]
            centered = value - lane_mean(value)
            rstd = lax.rsqrt(lane_mean(centered * centered) + 1e-05)
            xhat = centered * rstd
            xhat_s[at, :] = xhat.astype(bf16)
            normed_s[at, :] = (xhat * gain1_ref[...][None, :] + bias1_ref[...][None, :]).astype(
                bf16
            )
            rstd_s[at, :] = rstd
        group = pl.ds(pl.multiple_of(step * rows, 8), rows)
        middle_s[group, :] = emb_s[:rows, :]
        normed = normed_s[...]
        k_s[...] = dot(normed, w_qkv_ref[:, D : 2 * D]).astype(bf16)
        v_s[...] = (dot(normed, w_qkv_ref[:, 2 * D :]) + v_bias_ref[...][None, :]).astype(bf16)
        q_s[...] = (dot(normed[:rows], w_qkv_ref[:, :D]) + q_bias_ref[...][None, :]).astype(bf16)
        for copy in saves(step):
            copy.start()

        def attend(pair, carry):
            number = step * PAIRS + pair
            slot = lax.rem(number, SLOTS)
            at = pl.ds(pl.multiple_of(pair * PAIR, PAIR), PAIR)
            query = q_s[:, at]
            key = k_s[:, at]
            value = jnp.concatenate([v_s[:, at], jnp.ones((LEN, PAIR), bf16)], axis=1)
            parts = []
            for head in range(2):
                scores = dot_rt(jnp.where(own_lanes(head), query, jnp.zeros_like(query)), key)
                largest = jnp.max(scores, axis=1, keepdims=True)
                weights = jnp.exp2(
                    (scores - largest) * (HEAD**-0.5 * np.log2(np.e))
                ).astype(bf16)
                p_s[slot, head] = weights
                parts.append(dot(weights, value))
            first = own_lanes(0)
            inverse = 1.0 / jnp.where(first, parts[0][:, PAIR:], parts[1][:, PAIR:])
            linv_s[group, at] = inverse
            att_s[group, at] = jnp.where(first, parts[0][:, :PAIR], parts[1][:, :PAIR]) * inverse
            p_save(number).start()
            return carry

        lax.fori_loop(0, PAIRS, attend, 0, unroll=UNROLL_F)

    @pl.when(step == 0)
    def _():
        norms_ref[...] = jnp.zeros_like(norms_ref)
        norms_ref[0:1, :] = square_sum(w_proj_ref)
        norms_ref[4:5, :] = square_sum(w_qkv_ref)
        b_fc1_s[...] = b_fc1_ref[...][None, :]

    @pl.when(step == clips)
    def _():
        for copy in loads():
            copy.wait()
        attended_s[...] = att_s[...].astype(bf16)
        gn_s[...] = dot(attended_s[...], w_out_s[...])

        def norm_middle(at, carry):
            middle = middle_s[at, :] + (gn_s[at, :] + b_out_ref[...][None, :])
            centered = middle - lane_mean(middle)
            rstd = lax.rsqrt(lane_mean(centered * centered) + 1e-05)
            xhat = centered * rstd
            xhat2_s[at, :] = xhat
            rstd2_s[at, :] = rstd
            normed2_s[at, :] = (
                xhat * gain2_ref[...][None, :] + bias2_ref[...][None, :]
            ).astype(bf16)
            middle_s[at, :] = middle + b_fc2_ref[...][None, :]
            gn_s[at, :] = jnp.zeros(middle.shape, f32)
            return carry

        row_loop(clips * rows, norm_middle, 0, unroll=2)
        norms_ref[1:2, :] = square_sum(w_out_s)
        norms_ref[2:3, :] = square_sum(w_fc1_s)
        norms_ref[3:4, :] = square_sum(w_fc2_s)
        flat_s[FC_USED - 24 :, :] = jnp.zeros_like(flat_s[FC_USED - 24 :, :])

        def hidden_block(block, carry):
            normed2 = normed2_s[...]
            cot = cot_s[...]
            at = pl.ds(pl.multiple_of(block * BLOCK, BLOCK), BLOCK)
            w_fc1 = w_fc1_s[:, at]
            w_fc2 = w_fc2_s[at, :]
            pre = dot(normed2, w_fc1) + b_fc1_s[:, at]
            cdf = 0.5 + 0.5 * lax.erf(pre * np.float32(0.5**0.5))
            hidden = (pre * cdf).astype(bf16)
            slope = cdf + pre * (
                jnp.exp2(pre * pre * (-0.5 * np.log2(np.e))) * ((2 * np.pi) ** -0.5)
            )
            grad_pre = dot_rt(cot, w_fc2) * slope
            grad_pre_b = grad_pre.astype(bf16)
            middle_s[...] += dot(hidden, w_fc2)
            gn_s[...] += dot_rt(grad_pre_b, w_fc1)
            grad_w2 = dot_lt(hidden, cot).astype(bf16)
            for column in range(D // PAIR):
                first = FF * PAIRS + column * FF + block * BLOCK
                flat_s[pl.ds(pl.multiple_of(first, 16), BLOCK), :] = grad_w2[
                    :, column * PAIR : (column + 1) * PAIR
                ]
            grad_w1 = dot_lt(normed2, grad_pre_b).astype(bf16)
            sums = column_sums(grad_pre_b.astype(f32))
            for piece in range(BLOCK // PAIR):
                lanes = slice(piece * PAIR, (piece + 1) * PAIR)
                number = block * (BLOCK // PAIR) + piece
                flat_s[pl.ds(pl.multiple_of(number * D, 16), D), :] = grad_w1[:, lanes]
                row = 8 * lax.rem(number, PAIRS) + lax.div(number, PAIRS)
                vec_s[pl.ds(row, 1), :] = sums[:, lanes]
            return carry

        lax.fori_loop(0, BLOCKS, hidden_block, 0, unroll=UNROLL_M)
        out_s[...] = middle_s[...].astype(bf16)
        ends = [pltpu.make_async_copy(out_s, out_hbm, end_sems.at[0])]
        ends[0].start()

        def norm_back(at, carry):
            cot_f = cot_s[at, :].astype(f32)
            grad_normed = gn_s[at, :]
            xhat = xhat2_s[at, :]
            scaled = grad_normed * gain2_ref[...][None, :]
            grad_middle = cot_f + rstd2_s[at, :] * (
                scaled - lane_mean(scaled) - xhat * lane_mean(scaled * xhat)
            )
            middle_s[at, :] = grad_middle
            grad_branch = grad_middle.astype(bf16)
            normed2_s[at, :] = grad_branch
            terms = [cot_f, grad_normed * xhat, grad_normed, grad_branch.astype(f32)]
            return tuple(total + column_sums(term) for total, term in zip(carry, terms))

        zero = jnp.zeros((1, D), f32)
        vectors = row_loop(clips * rows, norm_back, (zero,) * 4, unroll=2)
        ends.append(pltpu.make_async_copy(middle_s, gmid_hbm, end_sems.at[1]))
        ends[1].start()
        grad_branch = normed2_s[...]
        grad_out = dot_lt(attended_s[...], grad_branch).astype(bf16)
        for column in range(D // PAIR):
            lanes = slice(column * PAIR, (column + 1) * PAIR)
            first = 2 * FF * PAIRS + column * D
            flat_s[first : first + D, :] = grad_out[:, lanes]
            for number, vector in enumerate(vectors):
                row = 8 * column + 4 + number
                vec_s[row : row + 1, :] = vector[:, lanes]
        flat_s[FC_USED - 24 : FC_USED, :] = vec_s[...].astype(bf16)
        bit = start_ref[1]
        for index, (side, target) in enumerate([(bit, kept_hbm), (1 - bit, sent_hbm)]):
            copy = pltpu.make_async_copy(
                flat_s.at[pl.ds(pl.multiple_of(side * half, 16), half)],
                target,
                end_sems.at[2 + index],
            )
            copy.start()
            ends.append(copy)
        gn_s[...] = dot_rt(grad_branch, w_out_s[...])

        def inner_products(at, carry):
            grad_att = gn_s[at, :].astype(bf16).astype(f32)
            grad_s = (grad_att * linv_s[at, :]).astype(bf16)
            gs_ref[at, :] = grad_s
            product = grad_s.astype(f32) * att_s[at, :]
            lane = lax.broadcasted_iota(jnp.int32, (1, PAIR), 1)
            packed = jnp.zeros((product.shape[0], PAIR), f32)
            for pair in range(PAIRS):
                piece = product[:, pair * PAIR : (pair + 1) * PAIR]
                for head in range(2):
                    inner = -jnp.sum(
                        jnp.where(own_lanes(head), piece, 0.0), axis=1, keepdims=True
                    )
                    for index, term in enumerate(split3(inner)):
                        where = 3 * (2 * pair + head) + index
                        packed = jnp.where(lane == where, term.astype(f32), packed)
            extra_ref[at, :] = packed.astype(bf16)
            return carry

        row_loop(clips * rows, inner_products, 0, unroll=2)
        for copy in ends + saves(clips - 1):
            copy.wait()
        for number in range(PAIRS * clips - PAIRS - 1, PAIRS * clips):
            p_save(number).wait()


def backward_kernel(
    start_ref,
    q_ref,
    k_ref,
    v_ref,
    gs_ref,
    extra_ref,
    x_ref,
    pos_ref,
    w_qkv_ref,
    gain1_ref,
    p_hbm,
    normed_hbm,
    xhat_hbm,
    rstd_hbm,
    gmid_hbm,
    *rest,
    rows,
    base,
    count,
    last,
):
    if last:
        acc_hbm, kept_ref, sent_ref, proj_kept_ref, proj_sent_ref = rest[:5]
        acc_s, total_sem = rest[5:7]
        scratch = rest[7:]
    else:
        acc_s, proj_kept_ref, proj_sent_ref = rest[:3]
        scratch = rest[3:]
    (p_s, normed_s, xhat_s, rstd_s, own_s, dq_s, dkv_s, gn_s, high_s, low_s, proj_s) = scratch[:-2]
    sems, p_sems = scratch[-2:]
    clip = pl.program_id(0)
    lane = lax.broadcasted_iota(jnp.int32, (1, PAIR), 1)

    def loads():
        at = base + clip
        pairs = [
            (normed_hbm.at[at], normed_s),
            (xhat_hbm.at[at], xhat_s),
            (rstd_hbm.at[at], rstd_s),
            (gmid_hbm.at[pl.ds(pl.multiple_of(at * rows, 8), rows)], own_s.at[pl.ds(0, rows)]),
        ]
        return [
            pltpu.make_async_copy(source, target, sems.at[index])
            for index, (source, target) in enumerate(pairs)
        ]

    def p_load(number):
        at = lax.div(number, PAIRS)
        pair = lax.rem(number, PAIRS)
        slot = lax.rem(number, 2 * PAIRS)
        return pltpu.make_async_copy(
            p_hbm.at[base + at, pl.ds(2 * pair, 2)], p_s.at[slot], p_sems.at[slot]
        )

    @pl.when(clip == 0)
    def _():
        for pair in range(PAIRS):
            p_load(pair).start()

    for copy in loads():
        copy.start()

    @pl.when(clip == 0)
    def _():
        own_s[rows:, :] = jnp.zeros_like(own_s[rows:, :])
        if last:
            pltpu.make_async_copy(acc_hbm, acc_s, total_sem).start()
        else:

            def clear(number, carry):
                at = pl.ds(pl.multiple_of(number * 256, 256), 256)
                acc_s[at, :] = jnp.zeros((256, PAIR), f32)
                return carry

            lax.fori_loop(0, acc_s.shape[0] // 256, clear, 0)

    def attend_back(phase, carry):
        number = clip * PAIRS + phase
        slot = lax.rem(number, 2 * PAIRS)
        p_load(number).wait()
        at = pl.ds(pl.multiple_of(phase * PAIR, PAIR), PAIR)
        query = q_ref[0, :, at] * jnp.asarray(HEAD**-0.5, bf16)
        key = k_ref[0, :, at]
        value = jnp.concatenate([v_ref[0, :, at], jnp.ones((LEN, PAIR), bf16)], axis=1)
        grad = gs_ref[:, at]
        extra = extra_ref[...]
        queries, keys, values = [], [], []
        for head in range(2):
            first = 3 * (2 * phase + head)
            inner = jnp.logical_and(lane >= first, lane < first + 3)
            left = jnp.concatenate(
                [
                    jnp.where(own_lanes(head), grad, jnp.zeros_like(grad)),
                    jnp.where(inner, extra, jnp.zeros_like(extra)),
                ],
                axis=1,
            )
            weights = p_s[slot, head]
            grad_scores = (weights.astype(f32) * dot_rt(left, value)).astype(bf16)
            queries.append(dot(grad_scores, key))
            keys.append(dot_lt(grad_scores, query))
            values.append(dot_lt(weights, grad))
        side = own_lanes(0)
        dq_s[:, at] = (jnp.where(side, queries[0], queries[1]) * (HEAD**-0.5)).astype(bf16)
        dkv_s[:, at] = jnp.where(side, keys[0], keys[1]).astype(bf16)
        at = pl.ds(pl.multiple_of(phase * PAIR + D, PAIR), PAIR)
        dkv_s[:, at] = jnp.where(side, values[0], values[1]).astype(bf16)
        return carry

    lax.fori_loop(0, PAIRS, attend_back, 0, unroll=UNROLL_B)

    @pl.when(clip + 1 < count)
    def _():
        for pair in range(PAIRS):
            p_load(PAIRS * (clip + 1) + pair).start()

    for copy in loads():
        copy.wait()
    if last:

        @pl.when(clip == 0)
        def _():
            pltpu.make_async_copy(acc_hbm, acc_s, total_sem).wait()

    if True:

        normed = normed_s[...]
        grad_q = dq_s[...]
        grad_kv = dkv_s[...]
        gn_s[...] = dot_rt(grad_kv, w_qkv_ref[:, D:])
        gn_s[:rows, :] += dot_rt(grad_q, w_qkv_ref[:, :D])
        part_q = dot_lt(normed[:rows], grad_q)
        part_kv = dot_lt(normed, grad_kv)
        for index in range(PAIRS):
            acc_s[index * D : (index + 1) * D, :] += part_q[:, index * PAIR : (index + 1) * PAIR]
        for index in range(2 * PAIRS):
            first = (PAIRS + index) * D
            acc_s[first : first + D, :] += part_kv[:, index * PAIR : (index + 1) * PAIR]
        ones = jnp.ones((8, LEN), bf16)
        sum_q = dot(ones[:, :rows], grad_q)[:1]
        sum_v = dot(ones, grad_kv[:, D:])[:1]

        def norm_rows(number, carry, with_own):
            at = pl.ds(pl.multiple_of(number * STEP, STEP), STEP)
            sum_gain, sum_bias, sum_emb = carry
            value = gn_s[at, :]
            xhat = xhat_s[at, :].astype(f32)
            sum_bias = sum_bias + column_sums(value)
            sum_gain = sum_gain + column_sums(value * xhat)
            scaled = value * gain1_ref[...][None, :]
            grad = rstd_s[at, :] * (
                scaled - lane_mean(scaled) - xhat * lane_mean(scaled * xhat)
            )
            if with_own:
                grad = grad + own_s[at, :]
            sum_emb = sum_emb + column_sums(grad)
            high = grad.astype(bf16)
            high_s[at, :] = high
            low_s[at, :] = (grad - high.astype(f32)).astype(bf16)
            return sum_gain, sum_bias, sum_emb

        zero = jnp.zeros((1, D), f32)
        own_steps = own_s.shape[0] // STEP
        carry = lax.fori_loop(
            0, own_steps, functools.partial(norm_rows, with_own=True), (zero, zero, zero), unroll=True
        )
        sum_gain, sum_bias, sum_emb = lax.fori_loop(
            own_steps, LEN // STEP, functools.partial(norm_rows, with_own=False), carry, unroll=True
        )
        row = lax.broadcasted_iota(jnp.int32, (LEN, 1), 0)
        onehot = (row == pos_ref[0]).astype(f32).astype(bf16)
        grad_proj = dot_lt(onehot, high_s[...]) + dot_lt(onehot, low_s[...])
        proj_s[...] = grad_proj
        bit = start_ref[1]
        part = SLOT // 2
        proj_kept_ref[0] = proj_s[pl.ds(pl.multiple_of(bit * part, 8), part), :]
        proj_sent_ref[0] = proj_s[
            pl.ds(pl.multiple_of((1 - bit) * part, 8), part), :
        ].astype(bf16)
        sum_proj = column_sums(grad_proj)
        vectors = [sum_proj, sum_emb - sum_proj, sum_gain, sum_bias, sum_q, sum_v]
        weight = dot_lt(x_ref[0], grad_proj[: x_ref.shape[1]].astype(bf16))
        for index in range(D // PAIR):
            lanes = slice(index * PAIR, (index + 1) * PAIR)
            first = 3 * PAIRS * D + index * DIN
            acc_s[first : first + DIN, :] += weight[:, lanes]
            first = 3 * PAIRS * D + PAIRS * DIN + 8 * index
            for number, vector in enumerate(vectors):
                acc_s[first + number : first + number + 1, :] += vector[:, lanes]

    if last:

        @pl.when(clip == count - 1)
        def _():
            bit = start_ref[1]
            half = kept_ref.shape[0]

            def hand_over(number, carry):
                at = pl.ds(pl.multiple_of(number * 256, 256), 256)
                kept_at = pl.ds(pl.multiple_of(bit * half + number * 256, 256), 256)
                sent_at = pl.ds(pl.multiple_of((1 - bit) * half + number * 256, 256), 256)
                kept_ref[at, :] = acc_s[kept_at, :]
                sent_ref[at, :] = acc_s[sent_at, :].astype(bf16)
                return carry

            lax.fori_loop(0, half // 256, hand_over, 0)


def place(target, lanes, source, where, total):
    size = target.shape[0]
    step = 96

    def move(number, total):
        first = pl.multiple_of(number * step, 16)
        value = source[pl.ds(pl.multiple_of(where + first, 16), step), :].astype(f32)
        target[pl.ds(first, step), lanes] = value
        return total + jnp.sum((value * value).reshape(step // 8, 8, PAIR), axis=0)

    return lax.fori_loop(0, size // step, move, total, unroll=2)


def lanes_of(index):
    return slice(index * PAIR, (index + 1) * PAIR)


def whole_mean(total, size):
    value = jnp.sum(jnp.sum(total, axis=1, keepdims=True), axis=0, keepdims=True)
    return value / size


def assemble_fc_kernel(
    start_ref,
    mine_hbm,
    other_hbm,
    w_out_ref,
    w_fc1_ref,
    w_fc2_ref,
    b_out_ref,
    gain_ref,
    bias_ref,
    b_fc1_ref,
    b_fc2_ref,
    mean_ref,
    full_s,
    sems,
):
    half = mine_hbm.shape[0]
    bit = start_ref[1]
    copies = [
        pltpu.make_async_copy(
            source, full_s.at[pl.ds(pl.multiple_of(side * half, 16), half)], sems.at[index]
        )
        for index, (source, side) in enumerate([(mine_hbm, bit), (other_hbm, 1 - bit)])
    ]
    for copy in copies:
        copy.start()
    for copy in copies:
        copy.wait()

    total = jnp.zeros((8, PAIR), f32)
    for index in range(PAIRS):
        total = place(w_out_ref, lanes_of(index), full_s, 2 * FF * PAIRS + index * D, total)
    mean_out = whole_mean(total, D * D)
    total = jnp.zeros((8, PAIR), f32)
    for index in range(FF // PAIR):
        total = place(w_fc1_ref, lanes_of(index), full_s, index * D, total)
    mean_fc1 = whole_mean(total, D * FF)
    total = jnp.zeros((8, PAIR), f32)
    for index in range(PAIRS):
        total = place(w_fc2_ref, lanes_of(index), full_s, FF * PAIRS + index * FF, total)
    mean_fc2 = whole_mean(total, FF * D)
    first = 2 * FF * PAIRS + PAIRS * D
    vectors = full_s[first : first + 24, :].astype(f32)
    for index in range(PAIRS):
        lanes = lanes_of(index)
        for number in range(4):
            b_fc1_ref[number * D + index * PAIR : number * D + (index + 1) * PAIR] = vectors[
                8 * index + number
            ]
        for number, target in enumerate([b_fc2_ref, gain_ref, bias_ref, b_out_ref]):
            target[lanes] = vectors[8 * index + 4 + number]
    row = lax.broadcasted_iota(jnp.int32, (8, PAIR), 0)
    mean_ref[...] = jnp.where(
        row == 1, mean_out, jnp.where(row == 2, mean_fc1, mean_fc2)
    )


def assemble_qkv_kernel(
    start_ref,
    *refs,
    far,
    chunk,
):
    planes = refs[:8]
    (
        norms_ref,
        mean_ref,
        w_proj_ref,
        w_qkv_ref,
        b_proj_ref,
        mask_ref,
        gain_ref,
        bias_ref,
        q_bias_ref,
        v_bias_ref,
        trust_ref,
        trust_qkv_ref,
        full_s,
        sems,
    ) = refs[8:]
    half = 4 * far * chunk
    bit = start_ref[1]
    copies = []
    for side in range(2):
        for plane in range(4):
            for line in range(far):
                place_at = jnp.bitwise_xor(start_ref[2], plane * far + line) * chunk
                place_at = place_at + (bit if side == 0 else 1 - bit) * half
                copies.append(
                    pltpu.make_async_copy(
                        planes[4 * side + plane].at[pl.ds(line * chunk, chunk)],
                        full_s.at[pl.ds(pl.multiple_of(place_at, 16), chunk)],
                        sems.at[len(copies)],
                    )
                )
    for copy in copies:
        copy.start()
    for copy in copies:
        copy.wait()

    total = jnp.zeros((8, PAIR), f32)
    for index in range(PAIRS):
        total = place(w_proj_ref, lanes_of(index), full_s, 3 * PAIRS * D + index * DIN, total)
    mean_proj = whole_mean(total, DIN * D)
    total = jnp.zeros((8, PAIR), f32)
    for index in range(3 * PAIRS):
        total = place(w_qkv_ref, lanes_of(index), full_s, index * D, total)
    mean_qkv = whole_mean(total, D * 3 * D)
    first = 3 * PAIRS * D + PAIRS * DIN
    vectors = full_s[first : first + 24, :].astype(f32)
    targets = [b_proj_ref, mask_ref, gain_ref, bias_ref, q_bias_ref, v_bias_ref]
    for index in range(PAIRS):
        for number, target in enumerate(targets):
            target[lanes_of(index)] = vectors[8 * index + number]
    lane = lax.broadcasted_iota(jnp.int32, (1, PAIR), 1)
    means = [mean_proj, mean_ref[1:2], mean_ref[2:3], mean_ref[3:4], mean_qkv]
    sums = jnp.sum(norms_ref[...], axis=1, keepdims=True)
    sizes = [DIN * D, D * D, D * FF, FF * D, D * 3 * D]
    grads = jnp.ones((1, PAIR), f32)
    weights = jnp.ones((1, PAIR), f32)
    for index, (mean, size) in enumerate(zip(means, sizes)):
        grads = jnp.where(lane == index, mean, grads)
        weights = jnp.where(lane == index, sums[index : index + 1] / size, weights)
    ratios = jnp.sqrt(weights) / jnp.sqrt(grads + 1e-06)
    trust_ref[...] = ratios[0, :4]
    trust_qkv_ref[...] = ratios[0, 4:5]


def whole(shape):
    return pl.BlockSpec(shape, lambda i, s: (0,) * len(shape), pipeline_mode=pl.Buffered(1))


def shape_of(shape, dtype):
    return jax.ShapeDtypeStruct(shape, dtype)


def kernel_call(kernel, grid, in_specs, out_specs, out_shape, scratch, name, cost, args):
    return pl.pallas_call(
        kernel,
        grid_spec=pltpu.PrefetchScalarGridSpec(
            num_scalar_prefetch=1,
            grid=grid,
            in_specs=in_specs,
            out_specs=out_specs,
            scratch_shapes=scratch,
        ),
        out_shape=out_shape,
        compiler_params=pltpu.CompilerParams(
            dimension_semantics=("arbitrary",), vmem_limit_bytes=VMEM
        ),
        cost_estimate=pl.CostEstimate(
            flops=cost[0], bytes_accessed=cost[1], transcendentals=cost[2]
        ),
        name=name,
    )(*args)


def run_forward(start, x_vis, padded_pos, table, params, cotangent, rows, half):
    clips, visible, _ = x_vis.shape
    (
        w_proj,
        b_proj,
        mask_token,
        ln1_gain,
        ln1_bias,
        w_qkv,
        q_bias,
        v_bias,
        w_out,
        b_out,
        ln2_gain,
        ln2_bias,
        w_fc1,
        b_fc1,
        w_fc2,
        b_fc2,
    ) = params
    tokens = clips * rows
    any_space = pl.BlockSpec(memory_space=pl.ANY)
    vector = whole((D,))

    def clip_at(i):
        return jnp.minimum(i, clips - 1)

    in_specs = [
        pl.BlockSpec((1, visible, DIN), lambda i, s: (clip_at(i), 0, 0)),
        pl.BlockSpec((1, 1, SLOT), lambda i, s: (clip_at(i), 0, 0)),
        pl.BlockSpec(
            (pl.Element(LEN // 8), pl.Element(8), pl.Element(D)),
            lambda i, s: (s[0], 0, 0),
            pipeline_mode=pl.Buffered(1),
        ),
        whole((DIN, D)),
        vector,
        vector,
        vector,
        vector,
        whole((D, 3 * D)),
        vector,
        vector,
        vector,
        vector,
        vector,
        whole((FF,)),
        vector,
    ] + [any_space] * 4
    out_specs = [whole((tokens, D)), whole((tokens, PAIR)), whole((8, PAIR))] + [any_space] * 11
    out_shape = [
        shape_of((tokens, D), bf16),
        shape_of((tokens, PAIR), bf16),
        shape_of((8, PAIR), f32),
        shape_of((tokens, D), bf16),
        shape_of((tokens, D), f32),
        shape_of((half, PAIR), bf16),
        shape_of((half, PAIR), bf16),
        shape_of((clips, HEADS, rows, LEN), bf16),
        shape_of((clips, rows, D), bf16),
        shape_of((clips, LEN, D), bf16),
        shape_of((clips, LEN, D), bf16),
        shape_of((clips, LEN, D), bf16),
        shape_of((clips, LEN, D), bf16),
        shape_of((clips, LEN, 1), f32),
    ]
    scratch = [
        pltpu.VMEM((SLOTS, 2, rows, LEN), bf16),
        pltpu.VMEM((rows, D), bf16),
        pltpu.VMEM((LEN, D), bf16),
        pltpu.VMEM((LEN, D), bf16),
        pltpu.VMEM((LEN, D), bf16),
        pltpu.VMEM((LEN, D), bf16),
        pltpu.VMEM((LEN, 1), f32),
        pltpu.VMEM((LEN, D), f32),
        pltpu.VMEM((tokens, D), f32),
        pltpu.VMEM((tokens, D), f32),
        pltpu.VMEM((tokens, D), f32),
        pltpu.VMEM((tokens, D), bf16),
        pltpu.VMEM((tokens, D), f32),
        pltpu.VMEM((tokens, 1), f32),
        pltpu.VMEM((tokens, D), bf16),
        pltpu.VMEM((tokens, D), f32),
        pltpu.VMEM((24, PAIR), f32),
        pltpu.VMEM((2 * half, PAIR), bf16),
        pltpu.VMEM((tokens, D), bf16),
        pltpu.VMEM((D, D), bf16),
        pltpu.VMEM((D, FF), bf16),
        pltpu.VMEM((FF, D), bf16),
        pltpu.VMEM((tokens, D), bf16),
        pltpu.VMEM((1, FF), f32),
        pltpu.SemaphoreType.DMA((6,)),
        pltpu.SemaphoreType.DMA((SLOTS,)),
        pltpu.SemaphoreType.DMA((4,)),
        pltpu.SemaphoreType.DMA((4,)),
    ]
    return kernel_call(
        functools.partial(forward_kernel, rows=rows, clips=clips),
        (clips + 1,),
        in_specs,
        out_specs,
        out_shape,
        scratch,
        "forward",
        (40_000_000_000, 60_000_000, 13_000_000),
        (
            start,
            x_vis,
            padded_pos,
            table,
            w_proj,
            b_proj,
            mask_token,
            ln1_gain,
            ln1_bias,
            w_qkv,
            q_bias,
            v_bias,
            b_out,
            ln2_gain,
            ln2_bias,
            b_fc1,
            b_fc2,
            w_out,
            w_fc1,
            w_fc2,
            cotangent.reshape(tokens, D),
        ),
    )


def run_backward(start, saved, x_vis, padded_pos, w_qkv, ln1_gain, rows, half, base, count, acc):
    query, key, value, grads, extra, weights, normed, xhat, rstd, gmid = saved
    _, visible, _ = x_vis.shape
    last = acc is not None
    own_rows = -(-rows // STEP) * STEP
    any_space = pl.BlockSpec(memory_space=pl.ANY)

    def at(i):
        return base + i

    def block(*shape):
        return pl.BlockSpec((1,) + shape, lambda i, s: (at(i),) + (0,) * len(shape))

    proj_spec = pl.BlockSpec((1, SLOT // 2, D), lambda i, s: (i, 0, 0))
    proj_shapes = [
        shape_of((count, SLOT // 2, D), f32),
        shape_of((count, SLOT // 2, D), bf16),
    ]
    in_specs = [
        block(rows, D),
        block(LEN, D),
        block(LEN, D),
        pl.BlockSpec((rows, D), lambda i, s: (at(i), 0)),
        pl.BlockSpec((rows, PAIR), lambda i, s: (at(i), 0)),
        block(visible, DIN),
        block(1, SLOT),
        whole((D, 3 * D)),
        whole((D,)),
    ] + [any_space] * 5
    args = [
        start,
        query,
        key,
        value,
        grads,
        extra,
        x_vis,
        padded_pos,
        w_qkv,
        ln1_gain,
        weights,
        normed,
        xhat,
        rstd,
        gmid,
    ]
    scratch = [
        pltpu.VMEM((2 * PAIRS, 2, rows, LEN), bf16),
        pltpu.VMEM((LEN, D), bf16),
        pltpu.VMEM((LEN, D), bf16),
        pltpu.VMEM((LEN, 1), f32),
        pltpu.VMEM((own_rows, D), f32),
        pltpu.VMEM((rows, D), bf16),
        pltpu.VMEM((LEN, 2 * D), bf16),
        pltpu.VMEM((LEN, D), f32),
        pltpu.VMEM((LEN, D), bf16),
        pltpu.VMEM((LEN, D), bf16),
        pltpu.VMEM((SLOT, D), f32),
        pltpu.SemaphoreType.DMA((4,)),
        pltpu.SemaphoreType.DMA((2 * PAIRS,)),
    ]
    if last:
        in_specs.append(any_space)
        args.append(acc)
        out_specs = [whole((half, PAIR)), whole((half, PAIR)), proj_spec, proj_spec]
        out_shape = [shape_of((half, PAIR), f32), shape_of((half, PAIR), bf16)] + proj_shapes
        scratch = [pltpu.VMEM((2 * half, PAIR), f32), pltpu.SemaphoreType.DMA] + scratch
    else:
        out_specs = [whole((2 * half, PAIR)), proj_spec, proj_spec]
        out_shape = [shape_of((2 * half, PAIR), f32)] + proj_shapes
    return kernel_call(
        functools.partial(backward_kernel, rows=rows, base=base, count=count, last=last),
        (count,),
        in_specs,
        out_specs,
        out_shape,
        scratch,
        "backward",
        (16_000_000_000 * count, 20_000_000 * count, 0),
        tuple(args),
    )


def run_assemble_fc(start, mine, other):
    half = mine.shape[0]
    shapes = [(D, D), (D, FF), (FF, D), (D,), (D,), (D,), (FF,), (D,), (8, PAIR)]
    return kernel_call(
        assemble_fc_kernel,
        (1,),
        [pl.BlockSpec(memory_space=pl.ANY)] * 2,
        [whole(size) for size in shapes],
        [shape_of(size, f32) for size in shapes],
        [pltpu.VMEM((2 * half, PAIR), bf16), pltpu.SemaphoreType.DMA((2,))],
        "assemble_fc",
        (10_000_000, 8_000_000, 0),
        (start, mine, other),
    )


def run_assemble_qkv(start, planes, norms, means, far, chunk):
    any_space = pl.BlockSpec(memory_space=pl.ANY)
    shapes = [(DIN, D), (D, 3 * D), (D,), (D,), (D,), (D,), (D,), (D,), (4,), (1,)]
    return kernel_call(
        functools.partial(assemble_qkv_kernel, far=far, chunk=chunk),
        (1,),
        [any_space] * 8 + [whole((8, PAIR)), whole((8, PAIR))],
        [whole(size) for size in shapes],
        [shape_of(size, f32) for size in shapes],
        [
            pltpu.VMEM((8 * far * chunk, PAIR), bf16),
            pltpu.SemaphoreType.DMA((8 * far,)),
        ],
        "assemble_qkv",
        (10_000_000, 5_000_000, 0),
        (start, *planes, norms, means),
    )


def add_received(kept, received):
    return kept.astype(f32) + received.astype(f32)


def shards(x_vis, vis_pos, *rest):
    params, cotangent = rest[:-1], rest[-1]
    w_proj, ln1_gain, w_qkv = params[0], params[3], params[5]
    seq_size = lax.axis_size("seq")
    clip_size = lax.axis_size("clip")
    groups = seq_size * clip_size // 2
    rows = LEN // seq_size
    clips, visible, _ = x_vis.shape
    far = clip_size // 2
    members = [
        [
            s * clip_size + 2 * high + low
            for s in range(core, seq_size, 2)
            for low in range(2)
            for high in range(far)
        ]
        for core in range(2)
    ]

    def chunk_rows(used):
        return -(-used // (32 * groups)) * 16

    core_pairs = [(s, s ^ 1) for s in range(seq_size)]
    chip_pairs = [(s, s ^ 2) for s in range(seq_size)]

    def across_core(value):
        return lax.ppermute(value, "seq", core_pairs)

    def swap(value):
        chunks = value.reshape(groups, -1, PAIR)
        return lax.all_to_all(chunks, AXES, 0, 0, axis_index_groups=members)

    def total_of(chunks):
        return jnp.sum(chunks.astype(f32), axis=0).astype(bf16)

    def spread(chunk, size):
        return jnp.broadcast_to(chunk[None], (size,) + chunk.shape)

    def across(value, seq_change, low_change, high_change):
        pairs = []
        for s in range(seq_size):
            for c in range(clip_size):
                other = (s ^ (2 * seq_change)) * clip_size + (c ^ (2 * high_change + low_change))
                pairs.append((s * clip_size + c, other))
        return lax.ppermute(value, AXES, pairs)

    def gather(chunk):
        size = 1
        while size < far:
            count = min(4, far // size)
            chunk = jnp.concatenate(
                [chunk] + [across(chunk, 0, 0, size * k) for k in range(1, count)]
            )
            size *= count
        return [chunk] + [across(chunk, k >> 1, k & 1, 0) for k in (1, 2, 3)]

    fc_chunk = chunk_rows(FC_USED)
    qkv_chunk = chunk_rows(QKV_USED)
    qkv_half = qkv_chunk * groups
    seq_index = lax.axis_index("seq")
    bit = seq_index & 1
    first = seq_index * rows
    local_pos = jnp.where(vis_pos >= first, vis_pos - first, vis_pos - first + LEN)
    padded_pos = jnp.pad(local_pos, ((0, 0), (0, SLOT - visible)), constant_values=-1)[:, None, :]
    table = sinusoid_table(LEN, D)
    table = jnp.asarray(np.concatenate([table, table[: LEN - rows]]).reshape(-1, 8, D))
    clip_index = lax.axis_index("clip")
    number = ((seq_index >> 1) * 2 + (clip_index & 1)) * far + (clip_index >> 1)
    start = jnp.stack([first // 8, bit, number]).astype(jnp.int32)

    (
        grads,
        extra,
        norms,
        output,
        gmid,
        kept,
        sent,
        weights,
        query,
        key,
        value,
        normed,
        xhat,
        rstd,
    ) = run_forward(start, x_vis, padded_pos, table, params, cotangent, rows, fc_chunk * groups)
    fc = add_received(kept, across_core(sent)).astype(bf16)
    fc, query = lax.optimization_barrier((fc, query))
    fc = swap(fc)
    saved = (query, key, value, grads, extra, weights, normed, xhat, rstd, gmid)
    acc, proj_kept0, proj_sent0 = run_backward(
        start, saved, x_vis, padded_pos, w_qkv, ln1_gain, rows, qkv_half, 0, clips - 1, None
    )
    fc, acc = lax.optimization_barrier((spread(total_of(fc), groups), acc))
    fc = swap(fc).reshape(groups * fc_chunk, PAIR)
    kept, sent, proj_kept1, proj_sent1 = run_backward(
        start, saved, x_vis, padded_pos, w_qkv, ln1_gain, rows, qkv_half, clips - 1, 1, acc
    )
    qkv = add_received(kept, across_core(sent)).astype(bf16)
    fc, qkv = lax.optimization_barrier((fc, qkv))
    qkv = swap(qkv)
    w_out_g, w_fc1_g, w_fc2_g, b_out_g, gain2_g, bias2_g, b_fc1_g, b_fc2_g, means = (
        run_assemble_fc(start, fc, across_core(fc))
    )
    qkv, means = lax.optimization_barrier((total_of(qkv), means))
    planes = gather(qkv)
    planes += [across_core(plane) for plane in planes]
    proj_kept = jnp.concatenate([proj_kept0, proj_kept1])
    proj_sent = jnp.concatenate([proj_sent0, proj_sent1])
    part = add_received(proj_kept, across_core(proj_sent)).astype(bf16)
    part = add_received(part, lax.ppermute(part, "seq", chip_pairs)).astype(bf16)
    other = across_core(part)
    grad_projected = jnp.where(
        bit == 0,
        jnp.concatenate([part, other], axis=1),
        jnp.concatenate([other, part], axis=1),
    )[:, :visible]
    grad_x = lax.dot_general(
        grad_projected, w_proj, (((2,), (1,)), ((), ())), preferred_element_type=f32
    )
    (
        w_proj_g,
        w_qkv_g,
        b_proj_g,
        mask_g,
        gain1_g,
        bias1_g,
        q_bias_g,
        v_bias_g,
        trust,
        trust_qkv,
    ) = run_assemble_qkv(start, planes, norms, means, far, qkv_chunk)
    return (
        output.reshape(clips, rows, D),
        grad_x,
        w_proj_g,
        b_proj_g,
        mask_g,
        gain1_g,
        bias1_g,
        w_qkv_g,
        q_bias_g,
        v_bias_g,
        w_out_g,
        b_out_g,
        gain2_g,
        bias2_g,
        w_fc1_g,
        b_fc1_g,
        w_fc2_g,
        b_fc2_g,
        trust,
        trust_qkv,
    )


def solution(mesh):
    return jax.shard_map(
        shards,
        mesh=mesh,
        in_specs=(P("clip", None, None), P("clip", None))
        + (P(),) * 16
        + (P("clip", "seq", None),),
        out_specs=(P("clip", "seq", None), P("clip", None, None)) + (P(),) * 18,
        check_vma=False,
    )
```

profile of v0, /device:TPU:1, one launch (start us, length us, event | category | flops | bytes accessed | tf_op | source)
XLA Modules:
  0.0 204.3 jit_solution(3748055216831923417)
XLA Ops:
  2.6 56.4 %forward.1 = (bf16[1176,384]{1,0:T(8,128)(2,1)}, bf16[1176,128]{1,0:T(8,128)(2,1)}, f32[8,128]{1,0:T(8,128)}, bf16[1176,384]{1,0:T(8,128)(2,1)}, f32[1176,384]{1...) custom-call(s32[3]{0:T(128)} %pad_add_fusion.start_ref, ...), custom_call_target="tpu_custom_call" | custom-call | flops 40000000000 | bytes 60000000 | tf_op jit(solution)/shard_map/forward/pallas_call | solution.py:789
  59.1 3.3 %collective-permute-done = bf16[5376,128]{1,0:T(8,128)(2,1)S(1)} collective-permute-done((bf16[5376,128]{1,0:T(8,128)(2,1)}, bf16[5376,128]{1,0:T(8,128)(2,1)S(1)}, u32[]{:S(2)}, u32[]{:S(2)}) %collective-permute-start) | collective-permute-done | bytes 1376288 | tf_op jit(solution)/shard_map/ppermute | solution.py:1088
  62.4 2.8 %add_convert_fusion = bf16[5376,128]{1,0:T(8,128)(2,1)} fusion(bf16[5376,128]{1,0:T(8,128)(2,1)S(1)} %collective-permute-done, bf16[5376,128]{1,0:T(8,128)(2,1)} %get-tuple-element.69), kind=kLoop, calls=%fused_computation | loop fusion | flops 2752512 | bytes 4128768 | tf_op jit(solution)/shard_map/convert_element_type | solution.py:1148
  65.1 7.7 %all-to-all-start = ((bf16[16,336,128]{2,1,0:T(8,128)(2,1)}), bf16[16,336,128]{2,1,0:T(8,128)(2,1)S(1)}, u32[]{:S(2)}, u32[]{:S(2)}) async-start(bf16[16,336,128]{2,1,0:T(8,128)(2,1)} %bitcast.5), calls=%async_computation | async-start | bytes 2752512 | tf_op jit(solution)/shard_map/all_to_all | solution.py:1092
  72.9 39.0 %backward.2 = (f32[6144,128]{1,0:T(8,128)}, f32[2,80,384]{2,1,0:T(8,128)}, bf16[2,80,384]{2,1,0:T(8,128)(2,1)}) custom-call(s32[3]{0:T(128)} %pad_add_fusion.start_ref, bf16[3,392,384]{2,1,0:T(8,128)(2,1)} %get-tuple-element.72.q_ref, bf16[3,1568,384]{2,1,0:T(8,128)(2,1)} %get-tuple-element.73.k_ref, bf16[3,1568,384]{2,1,0:T(8,128)(2,1)} %get-tuple-element.74.v_ref, ...), custom_call_target="tpu_custom_call" | custom-call | flops 32000000000 | bytes 40000000 | tf_op jit(solution)/shard_map/backward/pallas_call | solution.py:789
  113.3 6.3 %all-to-all-start.1 = ((bf16[16,336,128]{2,1,0:T(8,128)(2,1)}), bf16[16,336,128]{2,1,0:T(8,128)(2,1)S(1)}, u32[]{:S(2)}, u32[]{:S(2)}) async-start(bf16[16,336,128]{2,1,0:T(8,128)(2,1)} %broadcast_in_dim.10), calls=%async_computation.1 | async-start | bytes 2752512 | tf_op jit(solution)/shard_map/all_to_all | solution.py:1092
  119.6 22.9 %backward.3 = (f32[3072,128]{1,0:T(8,128)}, bf16[3072,128]{1,0:T(8,128)(2,1)}, f32[1,80,384]{2,1,0:T(8,128)}, bf16[1,80,384]{2,1,0:T(8,128)(2,1)}) custom-call(s32[3]{0:T(128)} %pad_add_fusion.start_ref, bf16[3,392,384]{2,1,0:T(8,128)(2,1)} %get-tuple-element.72.q_ref, bf16[3,1568,384]{2,1,0:T(8,128)(2,1)} %get-tuple-element.73.k_ref, ...), custom_call_target="tpu_custom_call" | custom-call | flops 16000000000 | bytes 20000000 | tf_op jit(solution)/shard_map/backward/pallas_call | solution.py:789
  142.6 1.3 collective-permute-start.4
  143.9 2.1 %collective-permute-done.4 = bf16[3072,128]{1,0:T(8,128)(2,1)S(1)} collective-permute-done((bf16[3072,128]{1,0:T(8,128)(2,1)}, bf16[3072,128]{1,0:T(8,128)(2,1)S(1)}, u32[]{:S(2)}, u32[]{:S(2)}) %collective-permute-start.4) | collective-permute-done | bytes 786464 | tf_op jit(solution)/shard_map/ppermute | solution.py:1088
  146.0 2.5 %add_convert_fusion.1 = bf16[3072,128]{1,0:T(8,128)(2,1)} fusion(f32[3072,128]{1,0:T(8,128)} %get-tuple-element.90, bf16[3072,128]{1,0:T(8,128)(2,1)S(1)} %collective-permute-done.4), kind=kLoop, calls=%fused_computation.1 | loop fusion | flops 1179648 | bytes 3145728 | tf_op jit(solution)/shard_map/convert_element_type | solution.py:1160
  148.5 4.8 %all-to-all-done.1 = bf16[16,336,128]{2,1,0:T(8,128)(2,1)S(1)} async-done(((bf16[16,336,128]{2,1,0:T(8,128)(2,1)}), bf16[16,336,128]{2,1,0:T(8,128)(2,1)S(1)}, u32[]{:S(2)}, u32[]{:S(2)}) %all-to-all-start.1) | async-done | bytes 1376288 | tf_op jit(solution)/shard_map/all_to_all | solution.py:1092
  153.3 3.8 %all-to-all-start.2 = ((bf16[16,192,128]{2,1,0:T(8,128)(2,1)}), bf16[16,192,128]{2,1,0:T(8,128)(2,1)S(1)}, u32[]{:S(2)}, u32[]{:S(2)}) async-start(bf16[16,192,128]{2,1,0:T(8,128)(2,1)} %bitcast.8), calls=%async_computation.2 | async-start | bytes 1572864 | tf_op jit(solution)/shard_map/all_to_all | solution.py:1092
  157.2 1.6 collective-permute-start.5
  159.8 2.0 collective-permute-done.1
  161.8 1.7 fusion.6
  163.5 1.5 collective-permute-start.2
  166.1 6.1 %assemble_fc.1 = (f32[384,384]{1,0:T(8,128)}, f32[384,1536]{1,0:T(8,128)}, f32[1536,384]{1,0:T(8,128)}, f32[384]{0:T(512)}, f32[384]{0:T(512)}, /*index=5*/f32[3...) custom-call(s32[3]{0:T(128)} %pad_add_fusion.start_ref, bf16[5376,128]{1,0:T(8,128)(2,1)} %bitcast.12, ...), custom_call_target="tpu_custom_call" | custom-call | flops 10000000 | bytes 8000000 | tf_op jit(solution)/shard_map/assemble_fc/pallas_call | solution.py:789
  172.3 5.9 %all-to-all-done.2 = bf16[16,192,128]{2,1,0:T(8,128)(2,1)S(1)} async-done(((bf16[16,192,128]{2,1,0:T(8,128)(2,1)}), bf16[16,192,128]{2,1,0:T(8,128)(2,1)S(1)}, u32[]{:S(2)}, u32[]{:S(2)}) %all-to-all-start.2) | async-done | bytes 786464 | tf_op jit(solution)/shard_map/all_to_all | solution.py:1092
  178.4 3.5 %collective-permute-start.6 = (bf16[192,128]{1,0:T(8,128)(2,1)S(1)}, bf16[192,128]{1,0:T(8,128)(2,1)S(1)}, u32[]{:S(2)}, u32[]{:S(2)}) collective-permute-start(bf16[192,128]{1,0:T(8,128)(2,1)S(1)} %reduce_sum.25), channel_id=1, source_target_pairs={{0,2},{1,3},{2,0},{3,1},{4,6},{5,7},{6,4},{7,5},{8,10},{9,11},{10,... | collective-permute-start | bytes 147464 | tf_op jit(solution)/shard_map/ppermute | solution.py:1106
  181.9 1.7 collective-permute-done.6
  187.5 3.8 %collective-permute-start.3 = (bf16[3,80,384]{2,1,0:T(8,128)(2,1)S(1)}, bf16[3,80,384]{2,1,0:T(8,128)(2,1)S(1)}, u32[]{:S(2)}, u32[]{:S(2)}) collective-permute-start(bf16[3,80,384]{2,1,0:T(8,128)(2,1)S(1)} %add_convert_fusion.2), channel_id=1, source_target_pairs={{0,8},{8,0},{16,24},{24,16},{1,9},{9,1},{17,25},{25,17},{2,10},{10... | collective-permute-start | bytes 552968 | tf_op jit(solution)/shard_map/ppermute | solution.py:1088
  191.4 2.8 %collective-permute-start.15 = (bf16[768,128]{1,0:T(8,128)(2,1)S(1)}, bf16[768,128]{1,0:T(8,128)(2,1)S(1)}, u32[]{:S(2)}, u32[]{:S(2)}) collective-permute-start(bf16[768,128]{1,0:T(8,128)(2,1)S(1)} %collective-permute-done.11.refs_3_), channel_id=1, source_target_pairs={{0,8},{8,0},{16,24},{24,16},{1,9},{9,1},{17,25},{25,17},{2,10},{10... | collective-permute-start | bytes 589832 | tf_op jit(solution)/shard_map/ppermute | solution.py:1088
  196.2 1.7 fusion
  198.8 5.2 %assemble_qkv.1 = (f32[768,384]{1,0:T(8,128)}, f32[384,1152]{1,0:T(8,128)}, f32[384]{0:T(512)}, f32[384]{0:T(512)}, f32[384]{0:T(512)}, /*index=5*/f32[384]{0:T(...) custom-call(s32[3]{0:T(128)} %pad_add_fusion.start_ref, bf16[768,128]{1,0:T(8,128)(2,1)} %copy-done.2, ...), custom_call_target="tpu_custom_call" | custom-call | flops 10000000 | bytes 5000000 | tf_op jit(solution)/shard_map/assemble_qkv/pallas_call | solution.py:789
  (58 shorter events, 12.6 us)
Async XLA Ops:
  59.0 3.4 %collective-permute-start = (bf16[5376,128]{1,0:T(8,128)(2,1)}, bf16[5376,128]{1,0:T(8,128)(2,1)S(1)}, u32[]{:S(2)}, u32[]{:S(2)}) collective-permute-start(bf16[5376,128]{1,0:T(8,128)(2,1)} %get-tuple-element.70), channel_id=1, source_target_pairs={{0,8},{8,0},{16,24},{24,16},{1,9},{9,1},{17,25},{25,17},{2,10},{10... | collective-permute-start | bytes 4128776 | tf_op jit(solution)/shard_map/ppermute | solution.py:1088
  65.1 46.7 %all-to-all-start = ((bf16[16,336,128]{2,1,0:T(8,128)(2,1)}), bf16[16,336,128]{2,1,0:T(8,128)(2,1)S(1)}, u32[]{:S(2)}, u32[]{:S(2)}) async-start(bf16[16,336,128]{2,1,0:T(8,128)(2,1)} %bitcast.5), calls=%async_computation | async-start | bytes 2752512 | tf_op jit(solution)/shard_map/all_to_all | solution.py:1092
  113.3 40.0 %all-to-all-start.1 = ((bf16[16,336,128]{2,1,0:T(8,128)(2,1)}), bf16[16,336,128]{2,1,0:T(8,128)(2,1)S(1)}, u32[]{:S(2)}, u32[]{:S(2)}) async-start(bf16[16,336,128]{2,1,0:T(8,128)(2,1)} %broadcast_in_dim.10), calls=%async_computation.1 | async-start | bytes 2752512 | tf_op jit(solution)/shard_map/all_to_all | solution.py:1092
  142.6 3.4 %collective-permute-start.4 = (bf16[3072,128]{1,0:T(8,128)(2,1)}, bf16[3072,128]{1,0:T(8,128)(2,1)S(1)}, u32[]{:S(2)}, u32[]{:S(2)}) collective-permute-start(bf16[3072,128]{1,0:T(8,128)(2,1)} %get-tuple-element.91), channel_id=1, source_target_pairs={{0,8},{8,0},{16,24},{24,16},{1,9},{9,1},{17,25},{25,17},{2,10},{10... | collective-permute-start | bytes 2359304 | tf_op jit(solution)/shard_map/ppermute | solution.py:1088
  153.3 11.7 %copy-start = (bf16[16,336,128]{2,1,0:T(8,128)(2,1)}, bf16[16,336,128]{2,1,0:T(8,128)(2,1)S(1)}, u32[]{:S(2)}) copy-start(bf16[16,336,128]{2,1,0:T(8,128)(2,1)S(1)} %all-to-all-done.1) | copy-start | bytes 4128772
  153.3 24.8 %all-to-all-start.2 = ((bf16[16,192,128]{2,1,0:T(8,128)(2,1)}), bf16[16,192,128]{2,1,0:T(8,128)(2,1)S(1)}, u32[]{:S(2)}, u32[]{:S(2)}) async-start(bf16[16,192,128]{2,1,0:T(8,128)(2,1)} %bitcast.8), calls=%async_computation.2 | async-start | bytes 1572864 | tf_op jit(solution)/shard_map/all_to_all | solution.py:1092
  157.2 7.9 %collective-permute-start.5 = (bf16[5376,128]{1,0:T(8,128)(2,1)S(1)}, bf16[5376,128]{1,0:T(8,128)(2,1)S(1)}, u32[]{:S(2)}, u32[]{:S(2)}) collective-permute-start(bf16[5376,128]{1,0:T(8,128)(2,1)S(1)} %bitcast.11), channel_id=1, source_target_pairs={{0,8},{8,0},{16,24},{24,16},{1,9},{9,1},{17,25},{25,17},{2,10},{10... | collective-permute-start | bytes 4128776 | tf_op jit(solution)/shard_map/ppermute | solution.py:1088
  159.7 2.1 %collective-permute-start.1 = (bf16[3,80,384]{2,1,0:T(8,128)(2,1)S(1)}, bf16[3,80,384]{2,1,0:T(8,128)(2,1)S(1)}, u32[]{:S(2)}, u32[]{:S(2)}) collective-permute-start(bf16[3,80,384]{2,1,0:T(8,128)(2,1)S(1)} %pad_maximum_fusion.3), channel_id=1, source_target_pairs={{0,8},{8,0},{16,24},{24,16},{1,9},{9,1},{17,25},{25,17},{2,10},{10... | collective-permute-start | bytes 552968 | tf_op jit(solution)/shard_map/ppermute | solution.py:1088
  163.5 22.9 %collective-permute-start.2 = (bf16[3,80,384]{2,1,0:T(8,128)(2,1)}, bf16[3,80,384]{2,1,0:T(8,128)(2,1)}, u32[]{:S(2)}, u32[]{:S(2)}) collective-permute-start(bf16[3,80,384]{2,1,0:T(8,128)(2,1)} %fusion.6), channel_id=1, source_target_pairs={{0,16},{8,24},{16,0},{24,8},{1,17},{9,25},{17,1},{25,9},{2,18},{10... | collective-permute-start | bytes 552968 | tf_op jit(solution)/shard_map/ppermute | solution.py:1172
  172.3 23.9 %copy-start.10 = (bf16[768,384]{1,0:T(8,128)(2,1)S(1)}, bf16[768,384]{1,0:T(8,128)(2,1)}, u32[]{:S(2)}) copy-start(bf16[768,384]{1,0:T(8,128)(2,1)} %w_proj_ref.1) | copy-start | bytes 1769476
  178.3 5.4 %collective-permute-start.8 = (bf16[192,128]{1,0:T(8,128)(2,1)S(1)}, bf16[192,128]{1,0:T(8,128)(2,1)S(1)}, u32[]{:S(2)}, u32[]{:S(2)}) collective-permute-start(bf16[192,128]{1,0:T(8,128)(2,1)S(1)} %reduce_sum.25), channel_id=1, source_target_pairs={{0,6},{1,7},{2,4},{3,5},{4,2},{5,3},{6,0},{7,1},{8,14},{9,15},{10,... | collective-permute-start | bytes 147464 | tf_op jit(solution)/shard_map/ppermute | solution.py:1106
  178.4 5.3 %collective-permute-start.7 = (bf16[192,128]{1,0:T(8,128)(2,1)S(1)}, bf16[192,128]{1,0:T(8,128)(2,1)S(1)}, u32[]{:S(2)}, u32[]{:S(2)}) collective-permute-start(bf16[192,128]{1,0:T(8,128)(2,1)S(1)} %reduce_sum.25), channel_id=1, source_target_pairs={{0,4},{1,5},{2,6},{3,7},{4,0},{5,1},{6,2},{7,3},{8,12},{9,13},{10,... | collective-permute-start | bytes 147464 | tf_op jit(solution)/shard_map/ppermute | solution.py:1106
  178.4 5.2 %collective-permute-start.6 = (bf16[192,128]{1,0:T(8,128)(2,1)S(1)}, bf16[192,128]{1,0:T(8,128)(2,1)S(1)}, u32[]{:S(2)}, u32[]{:S(2)}) collective-permute-start(bf16[192,128]{1,0:T(8,128)(2,1)S(1)} %reduce_sum.25), channel_id=1, source_target_pairs={{0,2},{1,3},{2,0},{3,1},{4,6},{5,7},{6,4},{7,5},{8,10},{9,11},{10,... | collective-permute-start | bytes 147464 | tf_op jit(solution)/shard_map/ppermute | solution.py:1106
  183.7 14.3 %copy-start.2 = (bf16[768,128]{1,0:T(8,128)(2,1)}, bf16[768,128]{1,0:T(8,128)(2,1)S(1)}, u32[]{:S(2)}) copy-start(bf16[768,128]{1,0:T(8,128)(2,1)S(1)} %constant_dynamic-update-slice_fusion.refs_0_) | copy-start | bytes 589828
  183.7 7.7 %collective-permute-start.11 = (bf16[768,128]{1,0:T(8,128)(2,1)S(1)}, bf16[768,128]{1,0:T(8,128)(2,1)S(1)}, u32[]{:S(2)}, u32[]{:S(2)}) collective-permute-start(bf16[768,128]{1,0:T(8,128)(2,1)S(1)} %constant_dynamic-update-slice_fusion.refs_0_), channel_id=1, source_target_pairs={{0,17},{1,16},{2,19},{3,18},{4,21},{5,20},{6,23},{7,22},{8,25},{9,... | collective-permute-start | bytes 589832 | tf_op jit(solution)/shard_map/ppermute | solution.py:1106
  185.0 9.2 %collective-permute-start.10 = (bf16[768,128]{1,0:T(8,128)(2,1)S(1)}, bf16[768,128]{1,0:T(8,128)(2,1)S(1)}, u32[]{:S(2)}, u32[]{:S(2)}) collective-permute-start(bf16[768,128]{1,0:T(8,128)(2,1)S(1)} %constant_dynamic-update-slice_fusion.refs_0_), channel_id=1, source_target_pairs={{0,16},{1,17},{2,18},{3,19},{4,20},{5,21},{6,22},{7,23},{8,24},{9,... | collective-permute-start | bytes 589832 | tf_op jit(solution)/shard_map/ppermute | solution.py:1106
  185.4 10.1 %collective-permute-start.9 = (bf16[768,128]{1,0:T(8,128)(2,1)S(1)}, bf16[768,128]{1,0:T(8,128)(2,1)S(1)}, u32[]{:S(2)}, u32[]{:S(2)}) collective-permute-start(bf16[768,128]{1,0:T(8,128)(2,1)S(1)} %constant_dynamic-update-slice_fusion.refs_0_), channel_id=1, source_target_pairs={{0,1},{1,0},{2,3},{3,2},{4,5},{5,4},{6,7},{7,6},{8,9},{9,8},{10,11... | collective-permute-start | bytes 589832 | tf_op jit(solution)/shard_map/ppermute | solution.py:1106
  187.5 8.7 %collective-permute-start.3 = (bf16[3,80,384]{2,1,0:T(8,128)(2,1)S(1)}, bf16[3,80,384]{2,1,0:T(8,128)(2,1)S(1)}, u32[]{:S(2)}, u32[]{:S(2)}) collective-permute-start(bf16[3,80,384]{2,1,0:T(8,128)(2,1)S(1)} %add_convert_fusion.2), channel_id=1, source_target_pairs={{0,8},{8,0},{16,24},{24,16},{1,9},{9,1},{17,25},{25,17},{2,10},{10... | collective-permute-start | bytes 552968 | tf_op jit(solution)/shard_map/ppermute | solution.py:1088
  191.3 6.6 %collective-permute-start.12 = (bf16[768,128]{1,0:T(8,128)(2,1)S(1)}, bf16[768,128]{1,0:T(8,128)(2,1)S(1)}, u32[]{:S(2)}, u32[]{:S(2)}) collective-permute-start(bf16[768,128]{1,0:T(8,128)(2,1)S(1)} %constant_dynamic-update-slice_fusion.refs_0_), channel_id=1, source_target_pairs={{0,8},{8,0},{16,24},{24,16},{1,9},{9,1},{17,25},{25,17},{2,10},{10... | collective-permute-start | bytes 589832 | tf_op jit(solution)/shard_map/ppermute | solution.py:1088
  191.4 6.6 %copy-start.3 = (bf16[768,128]{1,0:T(8,128)(2,1)}, bf16[768,128]{1,0:T(8,128)(2,1)S(1)}, u32[]{:S(2)}) copy-start(bf16[768,128]{1,0:T(8,128)(2,1)S(1)} %collective-permute-done.11.refs_3_) | copy-start | bytes 589828
  191.4 6.5 %collective-permute-start.15 = (bf16[768,128]{1,0:T(8,128)(2,1)S(1)}, bf16[768,128]{1,0:T(8,128)(2,1)S(1)}, u32[]{:S(2)}, u32[]{:S(2)}) collective-permute-start(bf16[768,128]{1,0:T(8,128)(2,1)S(1)} %collective-permute-done.11.refs_3_), channel_id=1, source_target_pairs={{0,8},{8,0},{16,24},{24,16},{1,9},{9,1},{17,25},{25,17},{2,10},{10... | collective-permute-start | bytes 589832 | tf_op jit(solution)/shard_map/ppermute | solution.py:1088
  194.2 3.8 %copy-start.4 = (bf16[768,128]{1,0:T(8,128)(2,1)}, bf16[768,128]{1,0:T(8,128)(2,1)S(1)}, u32[]{:S(2)}) copy-start(bf16[768,128]{1,0:T(8,128)(2,1)S(1)} %collective-permute-done.10.refs_2_) | copy-start | bytes 589828
  194.2 3.7 %collective-permute-start.14 = (bf16[768,128]{1,0:T(8,128)(2,1)S(1)}, bf16[768,128]{1,0:T(8,128)(2,1)S(1)}, u32[]{:S(2)}, u32[]{:S(2)}) collective-permute-start(bf16[768,128]{1,0:T(8,128)(2,1)S(1)} %collective-permute-done.10.refs_2_), channel_id=1, source_target_pairs={{0,8},{8,0},{16,24},{24,16},{1,9},{9,1},{17,25},{25,17},{2,10},{10... | collective-permute-start | bytes 589832 | tf_op jit(solution)/shard_map/ppermute | solution.py:1088
  195.4 2.5 %collective-permute-start.13 = (bf16[768,128]{1,0:T(8,128)(2,1)S(1)}, bf16[768,128]{1,0:T(8,128)(2,1)S(1)}, u32[]{:S(2)}, u32[]{:S(2)}) collective-permute-start(bf16[768,128]{1,0:T(8,128)(2,1)S(1)} %collective-permute-done.9.refs_1_), channel_id=1, source_target_pairs={{0,8},{8,0},{16,24},{24,16},{1,9},{9,1},{17,25},{25,17},{2,10},{10... | collective-permute-start | bytes 589832 | tf_op jit(solution)/shard_map/ppermute | solution.py:1088
  (6 other events, 6.8 us)
where the time goes:
time: 205 us; the launch traced here: 204 us
  Pallas kernels  130 us (63%)
  starting transfers between devices  37.5 us (18%)
  waiting for transfers between devices  19.9 us (10%)
  other arithmetic  10.6 us (5%)
  local copies, waits for them, and re-layouts  3.83 us (2%)
    pallas_call x5, Pallas kernels, kernel_call(): pl.pallas_call(kernel, grid_spec=pltpu.PrefetchScalarGridSpec(num_scalar_...  130 us
    all_to_all x3, starting transfers between devices, swap(): return lax.all_to_all(chunks, AXES, 0, 0, axis_index_groups=members)  17.9 us
    ppermute x9, starting transfers between devices, across_core(): return lax.ppermute(value, 'seq', core_pairs)  11.8 us
    all_to_all x3, waiting for transfers between devices, swap(): return lax.all_to_all(chunks, AXES, 0, 0, axis_index_groups=members)  10.8 us
    ppermute x9, waiting for transfers between devices, across_core(): return lax.ppermute(value, 'seq', core_pairs)  7.4 us
    ppermute x6, starting transfers between devices, across(): return lax.ppermute(value, AXES, pairs)  6.31 us
  transfers between devices with their start and end apart: 19, of which 6 were waited for; matrix products, arithmetic and copies ran while one was open for 4% of the time, Pallas kernels for 33%

commit v1 on v0

--- a/solution.py
+++ b/solution.py
@@ -21,9 +21,8 @@
 BLOCK = 256
 BLOCKS = FF // BLOCK
 SLOTS = 4
-UNROLL_F = True
+UNROLL_F = False
 UNROLL_M = False
-UNROLL_B = False
 FC_USED = 10392
 QKV_USED = 5784
 AXES = ("seq", "clip")
@@ -264,16 +263,19 @@
             query = q_s[:, at]
             key = k_s[:, at]
             value = jnp.concatenate([v_s[:, at], jnp.ones((LEN, PAIR), bf16)], axis=1)
-            parts = []
-            for head in range(2):
-                scores = dot_rt(jnp.where(own_lanes(head), query, jnp.zeros_like(query)), key)
+            first = own_lanes(0)
+            none = jnp.zeros_like(query)
+            both = [
+                dot_rt(jnp.where(first, query, none), key),
+                dot_rt(jnp.where(first, none, query), key),
+            ]
+            weights = []
+            for head, scores in enumerate(both):
                 largest = jnp.max(scores, axis=1, keepdims=True)
-                weights = jnp.exp2(
-                    (scores - largest) * (HEAD**-0.5 * np.log2(np.e))
-                ).astype(bf16)
-                p_s[slot, head] = weights
-                parts.append(dot(weights, value))
-            first = own_lanes(0)
+                scaled = (scores - largest) * (HEAD**-0.5 * np.log2(np.e))
+                weights.append(jnp.exp2(scaled).astype(bf16))
+                p_s[slot, head] = weights[head]
+            parts = [dot(weight, value) for weight in weights]
             inverse = 1.0 / jnp.where(first, parts[0][:, PAIR:], parts[1][:, PAIR:])
             linv_s[group, at] = inverse
             att_s[group, at] = jnp.where(first, parts[0][:, :PAIR], parts[1][:, :PAIR]) * inverse
@@ -310,7 +312,7 @@
             gn_s[at, :] = jnp.zeros(middle.shape, f32)
             return carry
 
-        row_loop(clips * rows, norm_middle, 0, unroll=2)
+        row_loop(clips * rows, norm_middle, 0, unroll=True)
         norms_ref[1:2, :] = square_sum(w_out_s)
         norms_ref[2:3, :] = square_sum(w_fc1_s)
         norms_ref[3:4, :] = square_sum(w_fc2_s)
@@ -323,12 +325,13 @@
             w_fc1 = w_fc1_s[:, at]
             w_fc2 = w_fc2_s[at, :]
             pre = dot(normed2, w_fc1) + b_fc1_s[:, at]
+            grad_hidden = dot_rt(cot, w_fc2)
             cdf = 0.5 + 0.5 * lax.erf(pre * np.float32(0.5**0.5))
             hidden = (pre * cdf).astype(bf16)
             slope = cdf + pre * (
                 jnp.exp2(pre * pre * (-0.5 * np.log2(np.e))) * ((2 * np.pi) ** -0.5)
             )
-            grad_pre = dot_rt(cot, w_fc2) * slope
+            grad_pre = grad_hidden * slope
             grad_pre_b = grad_pre.astype(bf16)
             middle_s[...] += dot(hidden, w_fc2)
             gn_s[...] += dot_rt(grad_pre_b, w_fc1)
@@ -368,7 +371,7 @@
             return tuple(total + column_sums(term) for total, term in zip(carry, terms))
 
         zero = jnp.zeros((1, D), f32)
-        vectors = row_loop(clips * rows, norm_back, (zero,) * 4, unroll=2)
+        vectors = row_loop(clips * rows, norm_back, (zero,) * 4, unroll=True)
         ends.append(pltpu.make_async_copy(middle_s, gmid_hbm, end_sems.at[1]))
         ends[1].start()
         grad_branch = normed2_s[...]
@@ -411,7 +414,7 @@
             extra_ref[at, :] = packed.astype(bf16)
             return carry
 
-        row_loop(clips * rows, inner_products, 0, unroll=2)
+        row_loop(clips * rows, inner_products, 0, unroll=True)
         for copy in ends + saves(clips - 1):
             copy.wait()
         for number in range(PAIRS * clips - PAIRS - 1, PAIRS * clips):
@@ -425,10 +428,10 @@
     v_ref,
     gs_ref,
     extra_ref,
-    x_ref,
     pos_ref,
-    w_qkv_ref,
     gain1_ref,
+    w_qkv_hbm,
+    x_hbm,
     p_hbm,
     normed_hbm,
     xhat_hbm,
@@ -441,29 +444,37 @@
     last,
 ):
     if last:
-        acc_hbm, kept_ref, sent_ref, proj_kept_ref, proj_sent_ref = rest[:5]
-        acc_s, total_sem = rest[5:7]
+        acc_hbm, dq_hbm, dkv_hbm, kept_ref, sent_ref, proj_kept_ref, proj_sent_ref = rest[:7]
         scratch = rest[7:]
     else:
-        acc_s, proj_kept_ref, proj_sent_ref = rest[:3]
-        scratch = rest[3:]
-    (p_s, normed_s, xhat_s, rstd_s, own_s, dq_s, dkv_s, gn_s, high_s, low_s, proj_s) = scratch[:-2]
-    sems, p_sems = scratch[-2:]
-    clip = pl.program_id(0)
+        proj_kept_ref, proj_sent_ref, acc_hbm, dq_hbm, dkv_hbm = rest[:5]
+        scratch = rest[5:]
+    (p_s, normed_s, xhat_s, rstd_s, own_s, dq_s, dkv_s, gn_s, high_s, low_s, proj_s) = scratch[:-7]
+    w_qkv_s, x_s, acc_s, hand_sems, w_sem, sems, p_sems = scratch[-7:]
+    step = pl.program_id(0)
     lane = lax.broadcasted_iota(jnp.int32, (1, PAIR), 1)
+    first_post = base - 1 if last else base
 
     def loads():
-        at = base + clip
+        at = first_post + step
         pairs = [
             (normed_hbm.at[at], normed_s),
             (xhat_hbm.at[at], xhat_s),
             (rstd_hbm.at[at], rstd_s),
+            (x_hbm.at[at], x_s),
             (gmid_hbm.at[pl.ds(pl.multiple_of(at * rows, 8), rows)], own_s.at[pl.ds(0, rows)]),
         ]
         return [
             pltpu.make_async_copy(source, target, sems.at[index])
             for index, (source, target) in enumerate(pairs)
         ]
+
+    def hand(number):
+        pairs = [(acc_s, acc_hbm), (dq_s, dq_hbm), (dkv_s, dkv_hbm)]
+        inside, outside = pairs[number]
+        if last:
+            return pltpu.make_async_copy(outside, inside, hand_sems.at[number])
+        return pltpu.make_async_copy(inside, outside, hand_sems.at[number])
 
     def p_load(number):
         at = lax.div(number, PAIRS)
@@ -473,19 +484,32 @@
             p_hbm.at[base + at, pl.ds(2 * pair, 2)], p_s.at[slot], p_sems.at[slot]
         )
 
-    @pl.when(clip == 0)
+    w_load = pltpu.make_async_copy(w_qkv_hbm, w_qkv_s, w_sem)
+    has_post = True if last else step < count - 1
+
+    if last:
+        for number in (2, 1):
+            pl.when(step == 0)(hand(number).start)
+
+    @pl.when(step == 0)
     def _():
-        for pair in range(PAIRS):
-            p_load(pair).start()
-
-    for copy in loads():
-        copy.start()
-
-    @pl.when(clip == 0)
+        if not last:
+            for pair in range(PAIRS):
+                p_load(pair).start()
+        w_load.start()
+
+    @pl.when(has_post)
+    def _():
+        for copy in loads():
+            copy.start()
+
+    @pl.when(step == 0)
     def _():
         own_s[rows:, :] = jnp.zeros_like(own_s[rows:, :])
         if last:
-            pltpu.make_async_copy(acc_hbm, acc_s, total_sem).start()
+            hand(0).start()
+            for pair in range(PAIRS):
+                p_load(pair).start()
         else:
 
             def clear(number, carry):
@@ -496,7 +520,7 @@
             lax.fori_loop(0, acc_s.shape[0] // 256, clear, 0)
 
     def attend_back(phase, carry):
-        number = clip * PAIRS + phase
+        number = phase if last else step * PAIRS + phase
         slot = lax.rem(number, 2 * PAIRS)
         p_load(number).wait()
         at = pl.ds(pl.multiple_of(phase * PAIR, PAIR), PAIR)
@@ -505,7 +529,7 @@
         value = jnp.concatenate([v_ref[0, :, at], jnp.ones((LEN, PAIR), bf16)], axis=1)
         grad = gs_ref[:, at]
         extra = extra_ref[...]
-        queries, keys, values = [], [], []
+        products = []
         for head in range(2):
             first = 3 * (2 * phase + head)
             inner = jnp.logical_and(lane >= first, lane < first + 3)
@@ -516,11 +540,15 @@
                 ],
                 axis=1,
             )
-            weights = p_s[slot, head]
-            grad_scores = (weights.astype(f32) * dot_rt(left, value)).astype(bf16)
-            queries.append(dot(grad_scores, key))
-            keys.append(dot_lt(grad_scores, query))
-            values.append(dot_lt(weights, grad))
+            products.append(dot_rt(left, value))
+        weights = [p_s[slot, head] for head in range(2)]
+        scores = [
+            (weight.astype(f32) * product).astype(bf16)
+            for weight, product in zip(weights, products)
+        ]
+        values = [dot_lt(weight, grad) for weight in weights]
+        keys = [dot_lt(score, query) for score in scores]
+        queries = [dot(score, key) for score in scores]
         side = own_lanes(0)
         dq_s[:, at] = (jnp.where(side, queries[0], queries[1]) * (HEAD**-0.5)).astype(bf16)
         dkv_s[:, at] = jnp.where(side, keys[0], keys[1]).astype(bf16)
@@ -528,28 +556,36 @@
         dkv_s[:, at] = jnp.where(side, values[0], values[1]).astype(bf16)
         return carry
 
-    lax.fori_loop(0, PAIRS, attend_back, 0, unroll=UNROLL_B)
-
-    @pl.when(clip + 1 < count)
+    if last:
+
+        @pl.when(step == 1)
+        def _():
+            lax.fori_loop(0, PAIRS, attend_back, 0)
+
+    else:
+        lax.fori_loop(0, PAIRS, attend_back, 0)
+
+        @pl.when(step + 1 < count)
+        def _():
+            for pair in range(PAIRS):
+                p_load(PAIRS * (step + 1) + pair).start()
+
+    @pl.when(step == 0)
     def _():
-        for pair in range(PAIRS):
-            p_load(PAIRS * (clip + 1) + pair).start()
-
-    for copy in loads():
-        copy.wait()
-    if last:
-
-        @pl.when(clip == 0)
-        def _():
-            pltpu.make_async_copy(acc_hbm, acc_s, total_sem).wait()
-
-    if True:
-
+        w_load.wait()
+        if last:
+            for number in range(3):
+                hand(number).wait()
+
+    @pl.when(has_post)
+    def _():
+        for copy in loads():
+            copy.wait()
         normed = normed_s[...]
         grad_q = dq_s[...]
         grad_kv = dkv_s[...]
-        gn_s[...] = dot_rt(grad_kv, w_qkv_ref[:, D:])
-        gn_s[:rows, :] += dot_rt(grad_q, w_qkv_ref[:, :D])
+        gn_s[...] = dot_rt(grad_kv, w_qkv_s[:, D:])
+        gn_s[:rows, :] += dot_rt(grad_q, w_qkv_s[:, :D])
         part_q = dot_lt(normed[:rows], grad_q)
         part_kv = dot_lt(normed, grad_kv)
         for index in range(PAIRS):
@@ -600,7 +636,7 @@
         ].astype(bf16)
         sum_proj = column_sums(grad_proj)
         vectors = [sum_proj, sum_emb - sum_proj, sum_gain, sum_bias, sum_q, sum_v]
-        weight = dot_lt(x_ref[0], grad_proj[: x_ref.shape[1]].astype(bf16))
+        weight = dot_lt(x_s[...], grad_proj[: x_s.shape[0]].astype(bf16))
         for index in range(D // PAIR):
             lanes = slice(index * PAIR, (index + 1) * PAIR)
             first = 3 * PAIRS * D + index * DIN
@@ -611,7 +647,7 @@
 
     if last:
 
-        @pl.when(clip == count - 1)
+        @pl.when(step == 1)
         def _():
             bit = start_ref[1]
             half = kept_ref.shape[0]
@@ -625,6 +661,16 @@
                 return carry
 
             lax.fori_loop(0, half // 256, hand_over, 0)
+
+    else:
+        pl.when(step == count - 2)(hand(0).start)
+
+        @pl.when(step == count - 1)
+        def _():
+            hand(1).start()
+            hand(2).start()
+            for number in range(3):
+                hand(number).wait()
 
 
 def place(target, lanes, source, where, total):
@@ -937,23 +983,31 @@
     )
 
 
-def run_backward(start, saved, x_vis, padded_pos, w_qkv, ln1_gain, rows, half, base, count, acc):
+def run_backward(start, saved, x_vis, padded_pos, w_qkv, ln1_gain, rows, half, base, count, handed):
     query, key, value, grads, extra, weights, normed, xhat, rstd, gmid = saved
     _, visible, _ = x_vis.shape
-    last = acc is not None
+    last = handed is not None
     own_rows = -(-rows // STEP) * STEP
     any_space = pl.BlockSpec(memory_space=pl.ANY)
+    posts = count + 1 if last else count - 1
 
     def at(i):
-        return base + i
+        return base if last else i
 
     def block(*shape):
         return pl.BlockSpec((1,) + shape, lambda i, s: (at(i),) + (0,) * len(shape))
 
-    proj_spec = pl.BlockSpec((1, SLOT // 2, D), lambda i, s: (i, 0, 0))
+    proj_spec = pl.BlockSpec(
+        (1, SLOT // 2, D), lambda i, s: (jnp.minimum(i, posts - 1), 0, 0)
+    )
     proj_shapes = [
-        shape_of((count, SLOT // 2, D), f32),
-        shape_of((count, SLOT // 2, D), bf16),
+        shape_of((posts, SLOT // 2, D), f32),
+        shape_of((posts, SLOT // 2, D), bf16),
+    ]
+    hand_shapes = [
+        shape_of((2 * half, PAIR), f32),
+        shape_of((rows, D), bf16),
+        shape_of((LEN, 2 * D), bf16),
     ]
     in_specs = [
         block(rows, D),
@@ -961,11 +1015,9 @@
         block(LEN, D),
         pl.BlockSpec((rows, D), lambda i, s: (at(i), 0)),
         pl.BlockSpec((rows, PAIR), lambda i, s: (at(i), 0)),
-        block(visible, DIN),
-        block(1, SLOT),
-        whole((D, 3 * D)),
+        pl.BlockSpec((1, 1, SLOT), lambda i, s: (base - 1 + i if last else i, 0, 0)),
         whole((D,)),
-    ] + [any_space] * 5
+    ] + [any_space] * 7
     args = [
         start,
         query,
@@ -973,10 +1025,10 @@
         value,
         grads,
         extra,
+        padded_pos,
+        ln1_gain,
+        w_qkv,
         x_vis,
-        padded_pos,
-        w_qkv,
-        ln1_gain,
         weights,
         normed,
         xhat,
@@ -995,21 +1047,25 @@
         pltpu.VMEM((LEN, D), bf16),
         pltpu.VMEM((LEN, D), bf16),
         pltpu.VMEM((SLOT, D), f32),
-        pltpu.SemaphoreType.DMA((4,)),
+        pltpu.VMEM((D, 3 * D), bf16),
+        pltpu.VMEM((visible, DIN), bf16),
+        pltpu.VMEM((2 * half, PAIR), f32),
+        pltpu.SemaphoreType.DMA((3,)),
+        pltpu.SemaphoreType.DMA,
+        pltpu.SemaphoreType.DMA((5,)),
         pltpu.SemaphoreType.DMA((2 * PAIRS,)),
     ]
     if last:
-        in_specs.append(any_space)
-        args.append(acc)
+        in_specs += [any_space] * 3
+        args += handed
         out_specs = [whole((half, PAIR)), whole((half, PAIR)), proj_spec, proj_spec]
         out_shape = [shape_of((half, PAIR), f32), shape_of((half, PAIR), bf16)] + proj_shapes
-        scratch = [pltpu.VMEM((2 * half, PAIR), f32), pltpu.SemaphoreType.DMA] + scratch
     else:
-        out_specs = [whole((2 * half, PAIR)), proj_spec, proj_spec]
-        out_shape = [shape_of((2 * half, PAIR), f32)] + proj_shapes
+        out_specs = [proj_spec, proj_spec] + [any_space] * 3
+        out_shape = proj_shapes + hand_shapes
     return kernel_call(
         functools.partial(backward_kernel, rows=rows, base=base, count=count, last=last),
-        (count,),
+        (posts if last else count,),
         in_specs,
         out_specs,
         out_shape,
@@ -1105,6 +1161,38 @@
                 pairs.append((s * clip_size + c, other))
         return lax.ppermute(value, AXES, pairs)
 
+    def parts_of(arrays, index, count):
+        size = arrays[0].shape[0] // count
+        result = []
+        for k in range(count):
+            first = jnp.bitwise_xor(index, k) * size
+            pieces = [lax.dynamic_slice_in_dim(value, first, size, 0) for value in arrays]
+            total = pieces[0].astype(f32)
+            for piece in pieces[1:]:
+                total = total + piece.astype(f32)
+            result.append(total if k == 0 else total.astype(bf16))
+        return result
+
+    def scatter(kept, received, beside):
+        x, y, high = seq_index >> 1, clip_index & 1, clip_index >> 1
+        own, *others = parts_of([kept, received], 2 * x + y, 4)
+        arrays = [own] + [
+            across(value, k >> 1, k & 1, 0) for k, value in enumerate(others, 1)
+        ]
+        arrays, beside = lax.optimization_barrier((arrays, beside))
+        size = far
+        while size > 1:
+            count = 2 if size == 2 or (size.bit_length() % 2 == 0) else 4
+            size //= count
+            own, *others = parts_of(arrays, (high // size) % count, count)
+            arrays = [own] + [
+                across(value, 0, 0, size * k) for k, value in enumerate(others, 1)
+            ]
+        total = arrays[0]
+        for value in arrays[1:]:
+            total = total + value.astype(f32)
+        return total.astype(bf16), beside
+
     def gather(chunk):
         size = 1
         while size < far:
@@ -1119,13 +1207,13 @@
     qkv_chunk = chunk_rows(QKV_USED)
     qkv_half = qkv_chunk * groups
     seq_index = lax.axis_index("seq")
+    clip_index = lax.axis_index("clip")
     bit = seq_index & 1
     first = seq_index * rows
     local_pos = jnp.where(vis_pos >= first, vis_pos - first, vis_pos - first + LEN)
     padded_pos = jnp.pad(local_pos, ((0, 0), (0, SLOT - visible)), constant_values=-1)[:, None, :]
     table = sinusoid_table(LEN, D)
     table = jnp.asarray(np.concatenate([table, table[: LEN - rows]]).reshape(-1, 8, D))
-    clip_index = lax.axis_index("clip")
     number = ((seq_index >> 1) * 2 + (clip_index & 1)) * far + (clip_index >> 1)
     start = jnp.stack([first // 8, bit, number]).astype(jnp.int32)
 
@@ -1149,21 +1237,19 @@
     fc, query = lax.optimization_barrier((fc, query))
     fc = swap(fc)
     saved = (query, key, value, grads, extra, weights, normed, xhat, rstd, gmid)
-    acc, proj_kept0, proj_sent0 = run_backward(
+    proj_kept0, proj_sent0, *handed = run_backward(
         start, saved, x_vis, padded_pos, w_qkv, ln1_gain, rows, qkv_half, 0, clips - 1, None
     )
-    fc, acc = lax.optimization_barrier((spread(total_of(fc), groups), acc))
+    fc, handed = lax.optimization_barrier((spread(total_of(fc), groups), handed))
     fc = swap(fc).reshape(groups * fc_chunk, PAIR)
     kept, sent, proj_kept1, proj_sent1 = run_backward(
-        start, saved, x_vis, padded_pos, w_qkv, ln1_gain, rows, qkv_half, clips - 1, 1, acc
-    )
-    qkv = add_received(kept, across_core(sent)).astype(bf16)
-    fc, qkv = lax.optimization_barrier((fc, qkv))
-    qkv = swap(qkv)
+        start, saved, x_vis, padded_pos, w_qkv, ln1_gain, rows, qkv_half, clips - 1, 1, handed
+    )
+    fc, received = lax.optimization_barrier((fc, across_core(sent)))
     w_out_g, w_fc1_g, w_fc2_g, b_out_g, gain2_g, bias2_g, b_fc1_g, b_fc2_g, means = (
         run_assemble_fc(start, fc, across_core(fc))
     )
-    qkv, means = lax.optimization_barrier((total_of(qkv), means))
+    qkv, means = scatter(kept, received, means)
     planes = gather(qkv)
     planes += [across_core(plane) for plane in planes]
     proj_kept = jnp.concatenate([proj_kept0, proj_kept1])

time: 205 us -> 199 us (0.971)
  waiting for transfers between devices: 19.9 us -> 10.5 us
  starting transfers between devices: 37.5 us -> 41.8 us
    all_to_all x3 -> x2, waiting for transfers between devices: 10.8 us -> 0.01 us  [swap(): return lax.all_to_all(chunks, AXES, 0, 0, axis_index_groups=members)]
    ppermute x6 -> x12, starting transfers between devices: 6.31 us -> 12 us  [across(): return lax.ppermute(value, AXES, pairs)]
    all_to_all x3 -> x2, starting transfers between devices: 17.9 us -> 14 us  [swap(): return lax.all_to_all(chunks, AXES, 0, 0, axis_index_groups=members)]
    ppermute x6 -> x12, waiting for transfers between devices: 1.72 us -> 4.98 us  [across(): return lax.ppermute(value, AXES, pairs)]
    ppermute x9, starting transfers between devices: 11.8 us -> 14.6 us  [across_core(): return lax.ppermute(value, 'seq', core_pairs)]
    convert_element_type x1 -> x3, other arithmetic: 2.49 us -> 4.45 us  [the longest x2 3.56 us: parts_of(): result.append(total if k == 0 else total.astype(bf16))]
  transfers between devices with their start and end apart: 19 -> 24, of which waited for: 6 -> 5; matrix products, arithmetic and copies ran while one was open for 4% -> 4% of each run, Pallas kernels for 33% -> 36%
where the time goes in v1:
time: 199 us; the launch traced here: 198 us
  Pallas kernels  129 us (65%)
  starting transfers between devices  41.8 us (21%)
  other arithmetic  10.5 us (5%)
  waiting for transfers between devices  10.5 us (5%)
  local copies, waits for them, and re-layouts  3.75 us (2%)
    pallas_call x5, Pallas kernels, kernel_call(): pl.pallas_call(kernel, grid_spec=pltpu.PrefetchScalarGridSpec(num_scalar_...  129 us
    ppermute x9, starting transfers between devices, across_core(): return lax.ppermute(value, 'seq', core_pairs)  14.6 us
    all_to_all x2, starting transfers between devices, swap(): return lax.all_to_all(chunks, AXES, 0, 0, axis_index_groups=members)  14 us
    ppermute x12, starting transfers between devices, across(): return lax.ppermute(value, AXES, pairs)  12 us
    ppermute x9, waiting for transfers between devices, across_core(): return lax.ppermute(value, 'seq', core_pairs)  5.55 us
    ppermute x12, waiting for transfers between devices, across(): return lax.ppermute(value, AXES, pairs)  4.98 us
  transfers between devices with their start and end apart: 24, of which 5 were waited for; matrix products, arithmetic and copies ran while one was open for 4% of the time, Pallas kernels for 36%

profile of v1, /device:TPU:1, one launch (start us, length us, event | category | flops | bytes accessed | tf_op | source)
XLA Modules:
  0.0 198.5 jit_solution(13050739426438431604)
XLA Ops:
  2.6 52.7 %forward.1 = (bf16[1176,384]{1,0:T(8,128)(2,1)}, bf16[1176,128]{1,0:T(8,128)(2,1)}, f32[8,128]{1,0:T(8,128)}, bf16[1176,384]{1,0:T(8,128)(2,1)}, f32[1176,384]{1...) custom-call(s32[3]{0:T(128)} %pad_add_fusion.start_ref, ...), custom_call_target="tpu_custom_call" | custom-call | flops 40000000000 | bytes 60000000 | tf_op jit(solution)/shard_map/forward/pallas_call | solution.py:835
  55.5 3.3 %collective-permute-done = bf16[5376,128]{1,0:T(8,128)(2,1)S(1)} collective-permute-done((bf16[5376,128]{1,0:T(8,128)(2,1)}, bf16[5376,128]{1,0:T(8,128)(2,1)S(1)}, u32[]{:S(2)}, u32[]{:S(2)}) %collective-permute-start) | collective-permute-done | bytes 1376288 | tf_op jit(solution)/shard_map/ppermute | solution.py:1144
  58.7 2.8 %add_convert_fusion = bf16[5376,128]{1,0:T(8,128)(2,1)} fusion(bf16[5376,128]{1,0:T(8,128)(2,1)S(1)} %collective-permute-done, bf16[5376,128]{1,0:T(8,128)(2,1)} %get-tuple-element.76), kind=kLoop, calls=%fused_computation | loop fusion | flops 2752512 | bytes 4128768 | tf_op jit(solution)/shard_map/convert_element_type | solution.py:1236
  61.5 7.7 %all-to-all-start = ((bf16[16,336,128]{2,1,0:T(8,128)(2,1)}), bf16[16,336,128]{2,1,0:T(8,128)(2,1)S(1)}, u32[]{:S(2)}, u32[]{:S(2)}) async-start(bf16[16,336,128]{2,1,0:T(8,128)(2,1)} %bitcast.5), calls=%async_computation | async-start | bytes 2752512 | tf_op jit(solution)/shard_map/all_to_all | solution.py:1148
  69.2 34.2 %backward.2 = (f32[1,80,384]{2,1,0:T(8,128)}, bf16[1,80,384]{2,1,0:T(8,128)(2,1)}, f32[6144,128]{1,0:T(8,128)}, bf16[392,384]{1,0:T(8,128)(2,1)}, bf16[1568,768]{1,0:T(8,128)(2,1)}) custom-call(s32[3]{0:T(128)} %pad_add_fusion.start_ref, bf16[3,392,384]{2,1,0:T(8,128)(2,1)} %get-tuple-element.79.q_ref, bf16[3,1568,384]{2,1,0:T(8,128)(2,1)} %get-tuple-element.80.k_ref, ...), custom_call_target="tpu_custom_call" | custom-call | flops 32000000000 | bytes 40000000 | tf_op jit(solution)/shard_map/backward/pallas_call | solution.py:835
  103.7 1.3 broadcast_in_dim.10
  104.9 6.3 %all-to-all-start.1 = ((bf16[16,336,128]{2,1,0:T(8,128)(2,1)}), bf16[16,336,128]{2,1,0:T(8,128)(2,1)S(1)}, u32[]{:S(2)}, u32[]{:S(2)}) async-start(bf16[16,336,128]{2,1,0:T(8,128)(2,1)} %broadcast_in_dim.10), calls=%async_computation.1 | async-start | bytes 2752512 | tf_op jit(solution)/shard_map/all_to_all | solution.py:1148
  111.3 30.7 %backward.3 = (f32[3072,128]{1,0:T(8,128)}, bf16[3072,128]{1,0:T(8,128)(2,1)}, f32[2,80,384]{2,1,0:T(8,128)}, bf16[2,80,384]{2,1,0:T(8,128)(2,1)}) custom-call(s32[3]{0:T(128)} %pad_add_fusion.start_ref, bf16[3,392,384]{2,1,0:T(8,128)(2,1)} %get-tuple-element.79.q_ref, bf16[3,1568,384]{2,1,0:T(8,128)(2,1)} %get-tuple-element.80.k_ref, ...), custom_call_target="tpu_custom_call" | custom-call | flops 16000000000 | bytes 20000000 | tf_op jit(solution)/shard_map/backward/pallas_call | solution.py:835
  142.0 1.3 collective-permute-start.4
  143.3 2.3 %collective-permute-done.4 = bf16[3072,128]{1,0:T(8,128)(2,1)} collective-permute-done((bf16[3072,128]{1,0:T(8,128)(2,1)}, bf16[3072,128]{1,0:T(8,128)(2,1)}, u32[]{:S(2)}, u32[]{:S(2)}) %collective-permute-start.4) | collective-permute-done | bytes 786464 | tf_op jit(solution)/shard_map/ppermute | solution.py:1144
  146.7 2.4 %add_convert_fusion.1 = (bf16[768,128]{1,0:T(8,128)(2,1)S(1)}, bf16[768,128]{1,0:T(8,128)(2,1)S(1)}, bf16[768,128]{1,0:T(8,128)(2,1)}, f32[768,128]{1,0:T(8,128)S(1)}) fusion(f32[3072,128]{1,0:T(8,128)} %get-tuple-element.100, s32[]{:T(128)S(6)} %select_n.71, bf16[3072,128]{1,0:T(8,128)(2,1)} %collective-permute-done.4, s32[]{:T(128)S(6)} %select_n.70, ...), kind=kLoop, calls=%fused_computation.3 | loop fusion | flops 1081344 | bytes 3342352 | tf_op jit(solution)/shard_map/convert_element_type | solution.py:1173
  152.5 1.3 collective-permute-start.1
  155.0 6.1 %assemble_fc.1 = (f32[384,384]{1,0:T(8,128)}, f32[384,1536]{1,0:T(8,128)}, f32[1536,384]{1,0:T(8,128)}, f32[384]{0:T(512)}, f32[384]{0:T(512)}, /*index=5*/f32[3...) custom-call(s32[3]{0:T(128)} %pad_add_fusion.start_ref, bf16[5376,128]{1,0:T(8,128)(2,1)} %bitcast.11, ...), custom_call_target="tpu_custom_call" | custom-call | flops 10000000 | bytes 8000000 | tf_op jit(solution)/shard_map/assemble_fc/pallas_call | solution.py:835
  162.3 1.8 collective-permute-start.10
  167.5 1.4 collective-permute-done.11
  170.3 1.9 collective-permute-start.13
  172.1 1.3 collective-permute-start.14
  174.1 2.9 %collective-permute-done.14 = bf16[192,128]{1,0:T(8,128)(2,1)S(1)} collective-permute-done((bf16[192,128]{1,0:T(8,128)(2,1)S(1)}, bf16[192,128]{1,0:T(8,128)(2,1)S(1)}, u32[]{:S(2)}, u32[]{:S(2)}) %collective-permute-start.14) | collective-permute-done | bytes 49184 | tf_op jit(solution)/shard_map/ppermute | solution.py:1162
  177.0 1.3 collective-permute-start.15
  179.8 4.8 %collective-permute-start.3 = (bf16[3,80,384]{2,1,0:T(8,128)(2,1)S(1)}, bf16[3,80,384]{2,1,0:T(8,128)(2,1)S(1)}, u32[]{:S(2)}, u32[]{:S(2)}) collective-permute-start(bf16[3,80,384]{2,1,0:T(8,128)(2,1)S(1)} %add_convert_fusion.4), channel_id=1, source_target_pairs={{0,8},{8,0},{16,24},{24,16},{1,9},{9,1},{17,25},{25,17},{2,10},{10... | collective-permute-start | bytes 552968 | tf_op jit(solution)/shard_map/ppermute | solution.py:1144
  184.7 3.0 %collective-permute-start.19 = (bf16[768,128]{1,0:T(8,128)(2,1)S(1)}, bf16[768,128]{1,0:T(8,128)(2,1)S(1)}, u32[]{:S(2)}, u32[]{:S(2)}) collective-permute-start(bf16[768,128]{1,0:T(8,128)(2,1)S(1)} %collective-permute-done.15.refs_1_), channel_id=1, source_target_pairs={{0,8},{8,0},{16,24},{24,16},{1,9},{9,1},{17,25},{25,17},{2,10},{10... | collective-permute-start | bytes 589832 | tf_op jit(solution)/shard_map/ppermute | solution.py:1144
  188.1 2.4 %collective-permute-start.21 = (bf16[768,128]{1,0:T(8,128)(2,1)S(1)}, bf16[768,128]{1,0:T(8,128)(2,1)S(1)}, u32[]{:S(2)}, u32[]{:S(2)}) collective-permute-start(bf16[768,128]{1,0:T(8,128)(2,1)S(1)} %collective-permute-done.17.refs_3_), channel_id=1, source_target_pairs={{0,8},{8,0},{16,24},{24,16},{1,9},{9,1},{17,25},{25,17},{2,10},{10... | collective-permute-start | bytes 589832 | tf_op jit(solution)/shard_map/ppermute | solution.py:1144
  190.5 1.7 fusion
  193.0 5.2 %assemble_qkv.1 = (f32[768,384]{1,0:T(8,128)}, f32[384,1152]{1,0:T(8,128)}, f32[384]{0:T(512)}, f32[384]{0:T(512)}, f32[384]{0:T(512)}, /*index=5*/f32[384]{0:T(...) custom-call(s32[3]{0:T(128)} %pad_add_fusion.start_ref, bf16[768,128]{1,0:T(8,128)(2,1)} %copy-done.2, ...), custom_call_target="tpu_custom_call" | custom-call | flops 10000000 | bytes 5000000 | tf_op jit(solution)/shard_map/assemble_qkv/pallas_call | solution.py:835
  (74 shorter events, 17.4 us)
Async XLA Ops:
  55.3 3.4 %collective-permute-start = (bf16[5376,128]{1,0:T(8,128)(2,1)}, bf16[5376,128]{1,0:T(8,128)(2,1)S(1)}, u32[]{:S(2)}, u32[]{:S(2)}) collective-permute-start(bf16[5376,128]{1,0:T(8,128)(2,1)} %get-tuple-element.77), channel_id=1, source_target_pairs={{0,8},{8,0},{16,24},{24,16},{1,9},{9,1},{17,25},{25,17},{2,10},{10... | collective-permute-start | bytes 4128776 | tf_op jit(solution)/shard_map/ppermute | solution.py:1144
  61.5 42.0 %all-to-all-start = ((bf16[16,336,128]{2,1,0:T(8,128)(2,1)}), bf16[16,336,128]{2,1,0:T(8,128)(2,1)S(1)}, u32[]{:S(2)}, u32[]{:S(2)}) async-start(bf16[16,336,128]{2,1,0:T(8,128)(2,1)} %bitcast.5), calls=%async_computation | async-start | bytes 2752512 | tf_op jit(solution)/shard_map/all_to_all | solution.py:1148
  104.9 40.6 %all-to-all-start.1 = ((bf16[16,336,128]{2,1,0:T(8,128)(2,1)}), bf16[16,336,128]{2,1,0:T(8,128)(2,1)S(1)}, u32[]{:S(2)}, u32[]{:S(2)}) async-start(bf16[16,336,128]{2,1,0:T(8,128)(2,1)} %broadcast_in_dim.10), calls=%async_computation.1 | async-start | bytes 2752512 | tf_op jit(solution)/shard_map/all_to_all | solution.py:1148
  142.0 3.5 %collective-permute-start.4 = (bf16[3072,128]{1,0:T(8,128)(2,1)}, bf16[3072,128]{1,0:T(8,128)(2,1)}, u32[]{:S(2)}, u32[]{:S(2)}) collective-permute-start(bf16[3072,128]{1,0:T(8,128)(2,1)} %get-tuple-element.102), channel_id=1, source_target_pairs={{0,8},{8,0},{16,24},{24,16},{1,9},{9,1},{17,25},{25,17},{2,10},{10... | collective-permute-start | bytes 2359304 | tf_op jit(solution)/shard_map/ppermute | solution.py:1144
  145.6 8.3 %collective-permute-start.8 = (bf16[5376,128]{1,0:T(8,128)(2,1)S(1)}, bf16[5376,128]{1,0:T(8,128)(2,1)S(1)}, u32[]{:S(2)}, u32[]{:S(2)}) collective-permute-start(bf16[5376,128]{1,0:T(8,128)(2,1)S(1)} %bitcast.10), channel_id=1, source_target_pairs={{0,8},{8,0},{16,24},{24,16},{1,9},{9,1},{17,25},{25,17},{2,10},{10... | collective-permute-start | bytes 4128776 | tf_op jit(solution)/shard_map/ppermute | solution.py:1144
  149.2 11.9 %collective-permute-start.5 = (bf16[768,128]{1,0:T(8,128)(2,1)}, bf16[768,128]{1,0:T(8,128)(2,1)}, u32[]{:S(2)}, u32[]{:S(2)}) collective-permute-start(bf16[768,128]{1,0:T(8,128)(2,1)} %get-tuple-element.132), channel_id=1, source_target_pairs={{0,1},{1,0},{2,3},{3,2},{4,5},{5,4},{6,7},{7,6},{8,9},{9,8},{10,11... | collective-permute-start | bytes 589832 | tf_op jit(solution)/shard_map/ppermute | solution.py:1162
  150.1 11.0 %collective-permute-start.6 = (bf16[768,128]{1,0:T(8,128)(2,1)S(1)}, bf16[768,128]{1,0:T(8,128)(2,1)}, u32[]{:S(2)}, u32[]{:S(2)}) collective-permute-start(bf16[768,128]{1,0:T(8,128)(2,1)S(1)} %get-tuple-element.131), channel_id=1, source_target_pairs={{0,16},{1,17},{2,18},{3,19},{4,20},{5,21},{6,22},{7,23},{8,24},{9,... | collective-permute-start | bytes 589832 | tf_op jit(solution)/shard_map/ppermute | solution.py:1162
  151.3 9.8 %collective-permute-start.7 = (bf16[768,128]{1,0:T(8,128)(2,1)S(1)}, bf16[768,128]{1,0:T(8,128)(2,1)}, u32[]{:S(2)}, u32[]{:S(2)}) collective-permute-start(bf16[768,128]{1,0:T(8,128)(2,1)S(1)} %get-tuple-element.130), channel_id=1, source_target_pairs={{0,17},{1,16},{2,19},{3,18},{4,21},{5,20},{6,23},{7,22},{8,25},{9,... | collective-permute-start | bytes 589832 | tf_op jit(solution)/shard_map/ppermute | solution.py:1162
  152.5 12.7 %collective-permute-start.1 = (bf16[3,80,384]{2,1,0:T(8,128)(2,1)}, bf16[3,80,384]{2,1,0:T(8,128)(2,1)}, u32[]{:S(2)}, u32[]{:S(2)}) collective-permute-start(bf16[3,80,384]{2,1,0:T(8,128)(2,1)} %pad_maximum_fusion.4), channel_id=1, source_target_pairs={{0,8},{8,0},{16,24},{24,16},{1,9},{9,1},{17,25},{25,17},{2,10},{10... | collective-permute-start | bytes 552968 | tf_op jit(solution)/shard_map/ppermute | solution.py:1144
  162.3 5.2 %collective-permute-start.10 = (bf16[192,128]{1,0:T(8,128)(2,1)S(1)}, bf16[192,128]{1,0:T(8,128)(2,1)S(1)}, u32[]{:S(2)}, u32[]{:S(2)}) collective-permute-start(bf16[192,128]{1,0:T(8,128)(2,1)S(1)} %get-tuple-element.136), channel_id=1, source_target_pairs={{0,4},{1,5},{2,6},{3,7},{4,0},{5,1},{6,2},{7,3},{8,12},{9,13},{10,... | collective-permute-start | bytes 147464 | tf_op jit(solution)/shard_map/ppermute | solution.py:1162
  164.1 4.8 %collective-permute-start.11 = (bf16[192,128]{1,0:T(8,128)(2,1)S(1)}, bf16[192,128]{1,0:T(8,128)(2,1)S(1)}, u32[]{:S(2)}, u32[]{:S(2)}) collective-permute-start(bf16[192,128]{1,0:T(8,128)(2,1)S(1)} %get-tuple-element.135), channel_id=1, source_target_pairs={{0,6},{1,7},{2,4},{3,5},{4,2},{5,3},{6,0},{7,1},{8,14},{9,15},{10,... | collective-permute-start | bytes 147464 | tf_op jit(solution)/shard_map/ppermute | solution.py:1162
  165.3 3.6 %collective-permute-start.9 = (bf16[192,128]{1,0:T(8,128)(2,1)S(1)}, bf16[192,128]{1,0:T(8,128)(2,1)S(1)}, u32[]{:S(2)}, u32[]{:S(2)}) collective-permute-start(bf16[192,128]{1,0:T(8,128)(2,1)S(1)} %get-tuple-element.134), channel_id=1, source_target_pairs={{0,2},{1,3},{2,0},{3,1},{4,6},{5,7},{6,4},{7,5},{8,10},{9,11},{10,... | collective-permute-start | bytes 147464 | tf_op jit(solution)/shard_map/ppermute | solution.py:1162
  166.2 13.5 %collective-permute-start.2 = (bf16[3,80,384]{2,1,0:T(8,128)(2,1)S(1)}, bf16[3,80,384]{2,1,0:T(8,128)(2,1)S(1)}, u32[]{:S(2)}, u32[]{:S(2)}) collective-permute-start(bf16[3,80,384]{2,1,0:T(8,128)(2,1)S(1)} %fusion.6), channel_id=1, source_target_pairs={{0,16},{8,24},{16,0},{24,8},{1,17},{9,25},{17,1},{25,9},{2,18},{10... | collective-permute-start | bytes 552968 | tf_op jit(solution)/shard_map/ppermute | solution.py:1258
  169.8 3.6 %collective-permute-start.12 = (bf16[192,128]{1,0:T(8,128)(2,1)S(1)}, bf16[192,128]{1,0:T(8,128)(2,1)S(1)}, u32[]{:S(2)}, u32[]{:S(2)}) collective-permute-start(bf16[192,128]{1,0:T(8,128)(2,1)S(1)} %add_convert_fusion.5), channel_id=1, source_target_pairs={{0,2},{1,3},{2,0},{3,1},{4,6},{5,7},{6,4},{7,5},{8,10},{9,11},{10,... | collective-permute-start | bytes 147464 | tf_op jit(solution)/shard_map/ppermute | solution.py:1162
  170.3 3.8 %collective-permute-start.13 = (bf16[192,128]{1,0:T(8,128)(2,1)S(1)}, bf16[192,128]{1,0:T(8,128)(2,1)S(1)}, u32[]{:S(2)}, u32[]{:S(2)}) collective-permute-start(bf16[192,128]{1,0:T(8,128)(2,1)S(1)} %add_convert_fusion.5), channel_id=1, source_target_pairs={{0,4},{1,5},{2,6},{3,7},{4,0},{5,1},{6,2},{7,3},{8,12},{9,13},{10,... | collective-permute-start | bytes 147464 | tf_op jit(solution)/shard_map/ppermute | solution.py:1162
  172.1 4.8 %collective-permute-start.14 = (bf16[192,128]{1,0:T(8,128)(2,1)S(1)}, bf16[192,128]{1,0:T(8,128)(2,1)S(1)}, u32[]{:S(2)}, u32[]{:S(2)}) collective-permute-start(bf16[192,128]{1,0:T(8,128)(2,1)S(1)} %add_convert_fusion.5), channel_id=1, source_target_pairs={{0,6},{1,7},{2,4},{3,5},{4,2},{5,3},{6,0},{7,1},{8,14},{9,15},{10,... | collective-permute-start | bytes 147464 | tf_op jit(solution)/shard_map/ppermute | solution.py:1162
  177.0 7.7 %collective-permute-start.15 = (bf16[768,128]{1,0:T(8,128)(2,1)S(1)}, bf16[768,128]{1,0:T(8,128)(2,1)S(1)}, u32[]{:S(2)}, u32[]{:S(2)}) collective-permute-start(bf16[768,128]{1,0:T(8,128)(2,1)S(1)} %pad_maximum_fusion.3.refs_0_), channel_id=1, source_target_pairs={{0,1},{1,0},{2,3},{3,2},{4,5},{5,4},{6,7},{7,6},{8,9},{9,8},{10,11... | collective-permute-start | bytes 589832 | tf_op jit(solution)/shard_map/ppermute | solution.py:1162
  178.2 9.4 %collective-permute-start.16 = (bf16[768,128]{1,0:T(8,128)(2,1)S(1)}, bf16[768,128]{1,0:T(8,128)(2,1)S(1)}, u32[]{:S(2)}, u32[]{:S(2)}) collective-permute-start(bf16[768,128]{1,0:T(8,128)(2,1)S(1)} %pad_maximum_fusion.3.refs_0_), channel_id=1, source_target_pairs={{0,16},{1,17},{2,18},{3,19},{4,20},{5,21},{6,22},{7,23},{8,24},{9,... | collective-permute-start | bytes 589832 | tf_op jit(solution)/shard_map/ppermute | solution.py:1162
  179.4 8.7 %collective-permute-start.17 = (bf16[768,128]{1,0:T(8,128)(2,1)S(1)}, bf16[768,128]{1,0:T(8,128)(2,1)S(1)}, u32[]{:S(2)}, u32[]{:S(2)}) collective-permute-start(bf16[768,128]{1,0:T(8,128)(2,1)S(1)} %pad_maximum_fusion.3.refs_0_), channel_id=1, source_target_pairs={{0,17},{1,16},{2,19},{3,18},{4,21},{5,20},{6,23},{7,22},{8,25},{9,... | collective-permute-start | bytes 589832 | tf_op jit(solution)/shard_map/ppermute | solution.py:1162
  179.8 10.7 %collective-permute-start.3 = (bf16[3,80,384]{2,1,0:T(8,128)(2,1)S(1)}, bf16[3,80,384]{2,1,0:T(8,128)(2,1)S(1)}, u32[]{:S(2)}, u32[]{:S(2)}) collective-permute-start(bf16[3,80,384]{2,1,0:T(8,128)(2,1)S(1)} %add_convert_fusion.4), channel_id=1, source_target_pairs={{0,8},{8,0},{16,24},{24,16},{1,9},{9,1},{17,25},{25,17},{2,10},{10... | collective-permute-start | bytes 552968 | tf_op jit(solution)/shard_map/ppermute | solution.py:1144
  184.6 7.6 %collective-permute-start.18 = (bf16[768,128]{1,0:T(8,128)(2,1)S(1)}, bf16[768,128]{1,0:T(8,128)(2,1)S(1)}, u32[]{:S(2)}, u32[]{:S(2)}) collective-permute-start(bf16[768,128]{1,0:T(8,128)(2,1)S(1)} %pad_maximum_fusion.3.refs_0_), channel_id=1, source_target_pairs={{0,8},{8,0},{16,24},{24,16},{1,9},{9,1},{17,25},{25,17},{2,10},{10... | collective-permute-start | bytes 589832 | tf_op jit(solution)/shard_map/ppermute | solution.py:1144
  184.7 7.5 %collective-permute-start.19 = (bf16[768,128]{1,0:T(8,128)(2,1)S(1)}, bf16[768,128]{1,0:T(8,128)(2,1)S(1)}, u32[]{:S(2)}, u32[]{:S(2)}) collective-permute-start(bf16[768,128]{1,0:T(8,128)(2,1)S(1)} %collective-permute-done.15.refs_1_), channel_id=1, source_target_pairs={{0,8},{8,0},{16,24},{24,16},{1,9},{9,1},{17,25},{25,17},{2,10},{10... | collective-permute-start | bytes 589832 | tf_op jit(solution)/shard_map/ppermute | solution.py:1144
  187.7 4.5 %collective-permute-start.20 = (bf16[768,128]{1,0:T(8,128)(2,1)S(1)}, bf16[768,128]{1,0:T(8,128)(2,1)S(1)}, u32[]{:S(2)}, u32[]{:S(2)}) collective-permute-start(bf16[768,128]{1,0:T(8,128)(2,1)S(1)} %collective-permute-done.16.refs_2_), channel_id=1, source_target_pairs={{0,8},{8,0},{16,24},{24,16},{1,9},{9,1},{17,25},{25,17},{2,10},{10... | collective-permute-start | bytes 589832 | tf_op jit(solution)/shard_map/ppermute | solution.py:1144
  188.1 4.1 %collective-permute-start.21 = (bf16[768,128]{1,0:T(8,128)(2,1)S(1)}, bf16[768,128]{1,0:T(8,128)(2,1)S(1)}, u32[]{:S(2)}, u32[]{:S(2)}) collective-permute-start(bf16[768,128]{1,0:T(8,128)(2,1)S(1)} %collective-permute-done.17.refs_3_), channel_id=1, source_target_pairs={{0,8},{8,0},{16,24},{24,16},{1,9},{9,1},{17,25},{25,17},{2,10},{10... | collective-permute-start | bytes 589832 | tf_op jit(solution)/shard_map/ppermute | solution.py:1144
  (15 other events, 101.6 us)

commit v2 on v1

--- a/solution.py
+++ b/solution.py
@@ -449,8 +449,17 @@
     else:
         proj_kept_ref, proj_sent_ref, acc_hbm, dq_hbm, dkv_hbm = rest[:5]
         scratch = rest[5:]
-    (p_s, normed_s, xhat_s, rstd_s, own_s, dq_s, dkv_s, gn_s, high_s, low_s, proj_s) = scratch[:-7]
+    (p_s, normed_s, xhat_s, rstd_s, own_s, dq_s, dkv_s, gn_s, high_s, low_s, proj_s) = scratch[-18:-7]
     w_qkv_s, x_s, acc_s, hand_sems, w_sem, sems, p_sems = scratch[-7:]
+    if last:
+        q_s, k_s, v_s, late_sems = scratch[:4]
+        late = [
+            pltpu.make_async_copy(source.at[pl.ds(base, 1)], target, late_sems.at[index])
+            for index, (source, target) in enumerate(
+                [(q_ref, q_s), (k_ref, k_s), (v_ref, v_s)]
+            )
+        ]
+        q_ref, k_ref, v_ref = q_s, k_s, v_s
     step = pl.program_id(0)
     lane = lax.broadcasted_iota(jnp.int32, (1, PAIR), 1)
     first_post = base - 1 if last else base
@@ -508,6 +517,8 @@
         own_s[rows:, :] = jnp.zeros_like(own_s[rows:, :])
         if last:
             hand(0).start()
+            for copy in late:
+                copy.start()
             for pair in range(PAIRS):
                 p_load(pair).start()
         else:
@@ -560,6 +571,8 @@
 
         @pl.when(step == 1)
         def _():
+            for copy in late:
+                copy.wait()
             lax.fori_loop(0, PAIRS, attend_back, 0)
 
     else:
@@ -574,18 +587,24 @@
     def _():
         w_load.wait()
         if last:
-            for number in range(3):
-                hand(number).wait()
+            hand(1).wait()
+            hand(2).wait()
 
     @pl.when(has_post)
     def _():
-        for copy in loads():
-            copy.wait()
-        normed = normed_s[...]
         grad_q = dq_s[...]
         grad_kv = dkv_s[...]
         gn_s[...] = dot_rt(grad_kv, w_qkv_s[:, D:])
         gn_s[:rows, :] += dot_rt(grad_q, w_qkv_s[:, :D])
+        for copy in loads():
+            copy.wait()
+        if last:
+
+            @pl.when(step == 0)
+            def _():
+                hand(0).wait()
+
+        normed = normed_s[...]
         part_q = dot_lt(normed[:rows], grad_q)
         part_kv = dot_lt(normed, grad_kv)
         for index in range(PAIRS):
@@ -1056,6 +1075,13 @@
         pltpu.SemaphoreType.DMA((2 * PAIRS,)),
     ]
     if last:
+        in_specs[:3] = [any_space] * 3
+        scratch = [
+            pltpu.VMEM((1, rows, D), bf16),
+            pltpu.VMEM((1, LEN, D), bf16),
+            pltpu.VMEM((1, LEN, D), bf16),
+            pltpu.SemaphoreType.DMA((3,)),
+        ] + scratch
         in_specs += [any_space] * 3
         args += handed
         out_specs = [whole((half, PAIR)), whole((half, PAIR)), proj_spec, proj_spec]

time: 199 us -> 198 us (level)
  transfers between devices with their start and end apart: 24 -> 24, of which waited for: 5 -> 6; matrix products, arithmetic and copies ran while one was open for 4% -> 4% of each run, Pallas kernels for 36% -> 36%
where the time goes in v2:
time: 198 us
  Pallas kernels  128 us (65%)
  starting transfers between devices  41.6 us (21%)
  waiting for transfers between devices  10.8 us (5%)
  other arithmetic  10.5 us (5%)
  local copies, waits for them, and re-layouts  3.75 us (2%)
    pallas_call x5, Pallas kernels, kernel_call(): pl.pallas_call(kernel, grid_spec=pltpu.PrefetchScalarGridSpec(num_scalar_...  128 us
    ppermute x9, starting transfers between devices, across_core(): return lax.ppermute(value, 'seq', core_pairs)  15.2 us
    all_to_all x2, starting transfers between devices, swap(): return lax.all_to_all(chunks, AXES, 0, 0, axis_index_groups=members)  14 us
    ppermute x12, starting transfers between devices, across(): return lax.ppermute(value, AXES, pairs)  11.7 us
    ppermute x9, waiting for transfers between devices, across_core(): return lax.ppermute(value, 'seq', core_pairs)  5.55 us
    ppermute x12, waiting for transfers between devices, across(): return lax.ppermute(value, AXES, pairs)  4.99 us
  transfers between devices with their start and end apart: 24, of which 6 were waited for; matrix products, arithmetic and copies ran while one was open for 4% of the time, Pallas kernels for 36%

profile of v2, /device:TPU:1, one launch (start us, length us, event | category | flops | bytes accessed | tf_op | source)
XLA Modules:
  0.0 197.7 jit_solution(7860092935587642548)
XLA Ops:
  2.6 52.7 %forward.1 = (bf16[1176,384]{1,0:T(8,128)(2,1)}, bf16[1176,128]{1,0:T(8,128)(2,1)}, f32[8,128]{1,0:T(8,128)}, bf16[1176,384]{1,0:T(8,128)(2,1)}, f32[1176,384]{1...) custom-call(s32[3]{0:T(128)} %pad_add_fusion.start_ref, ...), custom_call_target="tpu_custom_call" | custom-call | flops 40000000000 | bytes 60000000 | tf_op jit(solution)/shard_map/forward/pallas_call | solution.py:854
  55.5 3.3 %collective-permute-done = bf16[5376,128]{1,0:T(8,128)(2,1)S(1)} collective-permute-done((bf16[5376,128]{1,0:T(8,128)(2,1)}, bf16[5376,128]{1,0:T(8,128)(2,1)S(1)}, u32[]{:S(2)}, u32[]{:S(2)}) %collective-permute-start) | collective-permute-done | bytes 1376288 | tf_op jit(solution)/shard_map/ppermute | solution.py:1170
  58.7 2.8 %add_convert_fusion = bf16[5376,128]{1,0:T(8,128)(2,1)} fusion(bf16[5376,128]{1,0:T(8,128)(2,1)S(1)} %collective-permute-done, bf16[5376,128]{1,0:T(8,128)(2,1)} %get-tuple-element.76), kind=kLoop, calls=%fused_computation | loop fusion | flops 2752512 | bytes 4128768 | tf_op jit(solution)/shard_map/convert_element_type | solution.py:1262
  61.5 7.7 %all-to-all-start = ((bf16[16,336,128]{2,1,0:T(8,128)(2,1)}), bf16[16,336,128]{2,1,0:T(8,128)(2,1)S(1)}, u32[]{:S(2)}, u32[]{:S(2)}) async-start(bf16[16,336,128]{2,1,0:T(8,128)(2,1)} %bitcast.5), calls=%async_computation | async-start | bytes 2752512 | tf_op jit(solution)/shard_map/all_to_all | solution.py:1174
  69.2 34.3 %backward.2 = (f32[1,80,384]{2,1,0:T(8,128)}, bf16[1,80,384]{2,1,0:T(8,128)(2,1)}, f32[6144,128]{1,0:T(8,128)}, bf16[392,384]{1,0:T(8,128)(2,1)}, bf16[1568,768]{1,0:T(8,128)(2,1)}) custom-call(s32[3]{0:T(128)} %pad_add_fusion.start_ref, bf16[3,392,384]{2,1,0:T(8,128)(2,1)} %get-tuple-element.79.q_ref, bf16[3,1568,384]{2,1,0:T(8,128)(2,1)} %get-tuple-element.80.k_ref, ...), custom_call_target="tpu_custom_call" | custom-call | flops 32000000000 | bytes 40000000 | tf_op jit(solution)/shard_map/backward/pallas_call | solution.py:854
  103.7 1.3 broadcast_in_dim.10
  105.0 6.3 %all-to-all-start.1 = ((bf16[16,336,128]{2,1,0:T(8,128)(2,1)}), bf16[16,336,128]{2,1,0:T(8,128)(2,1)S(1)}, u32[]{:S(2)}, u32[]{:S(2)}) async-start(bf16[16,336,128]{2,1,0:T(8,128)(2,1)} %broadcast_in_dim.10), calls=%async_computation.1 | async-start | bytes 2752512 | tf_op jit(solution)/shard_map/all_to_all | solution.py:1174
  111.3 29.9 %backward.3 = (f32[3072,128]{1,0:T(8,128)}, bf16[3072,128]{1,0:T(8,128)(2,1)}, f32[2,80,384]{2,1,0:T(8,128)}, bf16[2,80,384]{2,1,0:T(8,128)(2,1)}) custom-call(s32[3]{0:T(128)} %pad_add_fusion.start_ref, bf16[3,392,384]{2,1,0:T(8,128)(2,1)} %get-tuple-element.79.q_ref, bf16[3,1568,384]{2,1,0:T(8,128)(2,1)} %get-tuple-element.80.k_ref, ...), custom_call_target="tpu_custom_call" | custom-call | flops 16000000000 | bytes 20000000 | tf_op jit(solution)/shard_map/backward/pallas_call | solution.py:854
  141.2 1.3 collective-permute-start.4
  142.5 2.3 %collective-permute-done.4 = bf16[3072,128]{1,0:T(8,128)(2,1)} collective-permute-done((bf16[3072,128]{1,0:T(8,128)(2,1)}, bf16[3072,128]{1,0:T(8,128)(2,1)}, u32[]{:S(2)}, u32[]{:S(2)}) %collective-permute-start.4) | collective-permute-done | bytes 786464 | tf_op jit(solution)/shard_map/ppermute | solution.py:1170
  145.0 1.8 collective-permute-start.8
  146.8 2.4 %add_convert_fusion.1 = (bf16[768,128]{1,0:T(8,128)(2,1)S(1)}, bf16[768,128]{1,0:T(8,128)(2,1)S(1)}, bf16[768,128]{1,0:T(8,128)(2,1)}, f32[768,128]{1,0:T(8,128)S(1)}) fusion(f32[3072,128]{1,0:T(8,128)} %get-tuple-element.100, s32[]{:T(128)S(6)} %select_n.71, bf16[3072,128]{1,0:T(8,128)(2,1)} %collective-permute-done.4, s32[]{:T(128)S(6)} %select_n.70, ...), kind=kLoop, calls=%fused_computation.3 | loop fusion | flops 1081344 | bytes 3342352 | tf_op jit(solution)/shard_map/convert_element_type | solution.py:1199
  150.5 1.3 collective-permute-start.7
  152.6 1.3 collective-permute-start.1
  155.0 6.1 %assemble_fc.1 = (f32[384,384]{1,0:T(8,128)}, f32[384,1536]{1,0:T(8,128)}, f32[1536,384]{1,0:T(8,128)}, f32[384]{0:T(512)}, f32[384]{0:T(512)}, /*index=5*/f32[3...) custom-call(s32[3]{0:T(128)} %pad_add_fusion.start_ref, bf16[5376,128]{1,0:T(8,128)(2,1)} %bitcast.11, ...), custom_call_target="tpu_custom_call" | custom-call | flops 10000000 | bytes 8000000 | tf_op jit(solution)/shard_map/assemble_fc/pallas_call | solution.py:854
  166.7 1.3 collective-permute-done.11
  169.7 1.7 collective-permute-start.13
  173.5 2.7 %collective-permute-done.14 = bf16[192,128]{1,0:T(8,128)(2,1)S(1)} collective-permute-done((bf16[192,128]{1,0:T(8,128)(2,1)S(1)}, bf16[192,128]{1,0:T(8,128)(2,1)S(1)}, u32[]{:S(2)}, u32[]{:S(2)}) %collective-permute-start.14) | collective-permute-done | bytes 49184 | tf_op jit(solution)/shard_map/ppermute | solution.py:1188
  176.2 1.2 collective-permute-start.15
  179.0 4.8 %collective-permute-start.3 = (bf16[3,80,384]{2,1,0:T(8,128)(2,1)S(1)}, bf16[3,80,384]{2,1,0:T(8,128)(2,1)S(1)}, u32[]{:S(2)}, u32[]{:S(2)}) collective-permute-start(bf16[3,80,384]{2,1,0:T(8,128)(2,1)S(1)} %add_convert_fusion.4), channel_id=1, source_target_pairs={{0,8},{8,0},{16,24},{24,16},{1,9},{9,1},{17,25},{25,17},{2,10},{10... | collective-permute-start | bytes 552968 | tf_op jit(solution)/shard_map/ppermute | solution.py:1170
  183.9 3.0 %collective-permute-start.19 = (bf16[768,128]{1,0:T(8,128)(2,1)S(1)}, bf16[768,128]{1,0:T(8,128)(2,1)S(1)}, u32[]{:S(2)}, u32[]{:S(2)}) collective-permute-start(bf16[768,128]{1,0:T(8,128)(2,1)S(1)} %collective-permute-done.15.refs_1_), channel_id=1, source_target_pairs={{0,8},{8,0},{16,24},{24,16},{1,9},{9,1},{17,25},{25,17},{2,10},{10... | collective-permute-start | bytes 589832 | tf_op jit(solution)/shard_map/ppermute | solution.py:1170
  187.3 2.4 %collective-permute-start.21 = (bf16[768,128]{1,0:T(8,128)(2,1)S(1)}, bf16[768,128]{1,0:T(8,128)(2,1)S(1)}, u32[]{:S(2)}, u32[]{:S(2)}) collective-permute-start(bf16[768,128]{1,0:T(8,128)(2,1)S(1)} %collective-permute-done.17.refs_3_), channel_id=1, source_target_pairs={{0,8},{8,0},{16,24},{24,16},{1,9},{9,1},{17,25},{25,17},{2,10},{10... | collective-permute-start | bytes 589832 | tf_op jit(solution)/shard_map/ppermute | solution.py:1170
  189.7 1.7 fusion
  192.2 5.2 %assemble_qkv.1 = (f32[768,384]{1,0:T(8,128)}, f32[384,1152]{1,0:T(8,128)}, f32[384]{0:T(512)}, f32[384]{0:T(512)}, f32[384]{0:T(512)}, /*index=5*/f32[384]{0:T(...) custom-call(s32[3]{0:T(128)} %pad_add_fusion.start_ref, bf16[768,128]{1,0:T(8,128)(2,1)} %copy-done.2, ...), custom_call_target="tpu_custom_call" | custom-call | flops 10000000 | bytes 5000000 | tf_op jit(solution)/shard_map/assemble_qkv/pallas_call | solution.py:854
  (74 shorter events, 17.8 us)
Async XLA Ops:
  55.3 3.4 %collective-permute-start = (bf16[5376,128]{1,0:T(8,128)(2,1)}, bf16[5376,128]{1,0:T(8,128)(2,1)S(1)}, u32[]{:S(2)}, u32[]{:S(2)}) collective-permute-start(bf16[5376,128]{1,0:T(8,128)(2,1)} %get-tuple-element.77), channel_id=1, source_target_pairs={{0,8},{8,0},{16,24},{24,16},{1,9},{9,1},{17,25},{25,17},{2,10},{10... | collective-permute-start | bytes 4128776 | tf_op jit(solution)/shard_map/ppermute | solution.py:1170
  61.5 42.0 %all-to-all-start = ((bf16[16,336,128]{2,1,0:T(8,128)(2,1)}), bf16[16,336,128]{2,1,0:T(8,128)(2,1)S(1)}, u32[]{:S(2)}, u32[]{:S(2)}) async-start(bf16[16,336,128]{2,1,0:T(8,128)(2,1)} %bitcast.5), calls=%async_computation | async-start | bytes 2752512 | tf_op jit(solution)/shard_map/all_to_all | solution.py:1174
  105.0 40.0 %all-to-all-start.1 = ((bf16[16,336,128]{2,1,0:T(8,128)(2,1)}), bf16[16,336,128]{2,1,0:T(8,128)(2,1)S(1)}, u32[]{:S(2)}, u32[]{:S(2)}) async-start(bf16[16,336,128]{2,1,0:T(8,128)(2,1)} %broadcast_in_dim.10), calls=%async_computation.1 | async-start | bytes 2752512 | tf_op jit(solution)/shard_map/all_to_all | solution.py:1174
  141.2 3.5 %collective-permute-start.4 = (bf16[3072,128]{1,0:T(8,128)(2,1)}, bf16[3072,128]{1,0:T(8,128)(2,1)}, u32[]{:S(2)}, u32[]{:S(2)}) collective-permute-start(bf16[3072,128]{1,0:T(8,128)(2,1)} %get-tuple-element.102), channel_id=1, source_target_pairs={{0,8},{8,0},{16,24},{24,16},{1,9},{9,1},{17,25},{25,17},{2,10},{10... | collective-permute-start | bytes 2359304 | tf_op jit(solution)/shard_map/ppermute | solution.py:1170
  145.0 8.9 %collective-permute-start.8 = (bf16[5376,128]{1,0:T(8,128)(2,1)S(1)}, bf16[5376,128]{1,0:T(8,128)(2,1)S(1)}, u32[]{:S(2)}, u32[]{:S(2)}) collective-permute-start(bf16[5376,128]{1,0:T(8,128)(2,1)S(1)} %bitcast.10), channel_id=1, source_target_pairs={{0,8},{8,0},{16,24},{24,16},{1,9},{9,1},{17,25},{25,17},{2,10},{10... | collective-permute-start | bytes 4128776 | tf_op jit(solution)/shard_map/ppermute | solution.py:1170
  149.2 11.9 %collective-permute-start.5 = (bf16[768,128]{1,0:T(8,128)(2,1)}, bf16[768,128]{1,0:T(8,128)(2,1)}, u32[]{:S(2)}, u32[]{:S(2)}) collective-permute-start(bf16[768,128]{1,0:T(8,128)(2,1)} %get-tuple-element.132), channel_id=1, source_target_pairs={{0,1},{1,0},{2,3},{3,2},{4,5},{5,4},{6,7},{7,6},{8,9},{9,8},{10,11... | collective-permute-start | bytes 589832 | tf_op jit(solution)/shard_map/ppermute | solution.py:1188
  149.3 11.8 %collective-permute-start.6 = (bf16[768,128]{1,0:T(8,128)(2,1)S(1)}, bf16[768,128]{1,0:T(8,128)(2,1)}, u32[]{:S(2)}, u32[]{:S(2)}) collective-permute-start(bf16[768,128]{1,0:T(8,128)(2,1)S(1)} %get-tuple-element.131), channel_id=1, source_target_pairs={{0,16},{1,17},{2,18},{3,19},{4,20},{5,21},{6,22},{7,23},{8,24},{9,... | collective-permute-start | bytes 589832 | tf_op jit(solution)/shard_map/ppermute | solution.py:1188
  150.5 10.7 %collective-permute-start.7 = (bf16[768,128]{1,0:T(8,128)(2,1)S(1)}, bf16[768,128]{1,0:T(8,128)(2,1)}, u32[]{:S(2)}, u32[]{:S(2)}) collective-permute-start(bf16[768,128]{1,0:T(8,128)(2,1)S(1)} %get-tuple-element.130), channel_id=1, source_target_pairs={{0,17},{1,16},{2,19},{3,18},{4,21},{5,20},{6,23},{7,22},{8,25},{9,... | collective-permute-start | bytes 589832 | tf_op jit(solution)/shard_map/ppermute | solution.py:1188
  152.6 12.5 %collective-permute-start.1 = (bf16[3,80,384]{2,1,0:T(8,128)(2,1)}, bf16[3,80,384]{2,1,0:T(8,128)(2,1)}, u32[]{:S(2)}, u32[]{:S(2)}) collective-permute-start(bf16[3,80,384]{2,1,0:T(8,128)(2,1)} %pad_maximum_fusion.4), channel_id=1, source_target_pairs={{0,8},{8,0},{16,24},{24,16},{1,9},{9,1},{17,25},{25,17},{2,10},{10... | collective-permute-start | bytes 552968 | tf_op jit(solution)/shard_map/ppermute | solution.py:1170
  162.3 4.4 %collective-permute-start.10 = (bf16[192,128]{1,0:T(8,128)(2,1)S(1)}, bf16[192,128]{1,0:T(8,128)(2,1)S(1)}, u32[]{:S(2)}, u32[]{:S(2)}) collective-permute-start(bf16[192,128]{1,0:T(8,128)(2,1)S(1)} %get-tuple-element.136), channel_id=1, source_target_pairs={{0,4},{1,5},{2,6},{3,7},{4,0},{5,1},{6,2},{7,3},{8,12},{9,13},{10,... | collective-permute-start | bytes 147464 | tf_op jit(solution)/shard_map/ppermute | solution.py:1188
  163.3 4.7 %collective-permute-start.11 = (bf16[192,128]{1,0:T(8,128)(2,1)S(1)}, bf16[192,128]{1,0:T(8,128)(2,1)S(1)}, u32[]{:S(2)}, u32[]{:S(2)}) collective-permute-start(bf16[192,128]{1,0:T(8,128)(2,1)S(1)} %get-tuple-element.135), channel_id=1, source_target_pairs={{0,6},{1,7},{2,4},{3,5},{4,2},{5,3},{6,0},{7,1},{8,14},{9,15},{10,... | collective-permute-start | bytes 147464 | tf_op jit(solution)/shard_map/ppermute | solution.py:1188
  164.4 3.6 %collective-permute-start.9 = (bf16[192,128]{1,0:T(8,128)(2,1)S(1)}, bf16[192,128]{1,0:T(8,128)(2,1)S(1)}, u32[]{:S(2)}, u32[]{:S(2)}) collective-permute-start(bf16[192,128]{1,0:T(8,128)(2,1)S(1)} %get-tuple-element.134), channel_id=1, source_target_pairs={{0,2},{1,3},{2,0},{3,1},{4,6},{5,7},{6,4},{7,5},{8,10},{9,11},{10,... | collective-permute-start | bytes 147464 | tf_op jit(solution)/shard_map/ppermute | solution.py:1188
  166.0 12.9 %collective-permute-start.2 = (bf16[3,80,384]{2,1,0:T(8,128)(2,1)S(1)}, bf16[3,80,384]{2,1,0:T(8,128)(2,1)S(1)}, u32[]{:S(2)}, u32[]{:S(2)}) collective-permute-start(bf16[3,80,384]{2,1,0:T(8,128)(2,1)S(1)} %fusion.6), channel_id=1, source_target_pairs={{0,16},{8,24},{16,0},{24,8},{1,17},{9,25},{17,1},{25,9},{2,18},{10... | collective-permute-start | bytes 552968 | tf_op jit(solution)/shard_map/ppermute | solution.py:1284
  168.9 3.6 %collective-permute-start.12 = (bf16[192,128]{1,0:T(8,128)(2,1)S(1)}, bf16[192,128]{1,0:T(8,128)(2,1)S(1)}, u32[]{:S(2)}, u32[]{:S(2)}) collective-permute-start(bf16[192,128]{1,0:T(8,128)(2,1)S(1)} %add_convert_fusion.5), channel_id=1, source_target_pairs={{0,2},{1,3},{2,0},{3,1},{4,6},{5,7},{6,4},{7,5},{8,10},{9,11},{10,... | collective-permute-start | bytes 147464 | tf_op jit(solution)/shard_map/ppermute | solution.py:1188
  169.7 3.8 %collective-permute-start.13 = (bf16[192,128]{1,0:T(8,128)(2,1)S(1)}, bf16[192,128]{1,0:T(8,128)(2,1)S(1)}, u32[]{:S(2)}, u32[]{:S(2)}) collective-permute-start(bf16[192,128]{1,0:T(8,128)(2,1)S(1)} %add_convert_fusion.5), channel_id=1, source_target_pairs={{0,4},{1,5},{2,6},{3,7},{4,0},{5,1},{6,2},{7,3},{8,12},{9,13},{10,... | collective-permute-start | bytes 147464 | tf_op jit(solution)/shard_map/ppermute | solution.py:1188
  171.3 4.8 %collective-permute-start.14 = (bf16[192,128]{1,0:T(8,128)(2,1)S(1)}, bf16[192,128]{1,0:T(8,128)(2,1)S(1)}, u32[]{:S(2)}, u32[]{:S(2)}) collective-permute-start(bf16[192,128]{1,0:T(8,128)(2,1)S(1)} %add_convert_fusion.5), channel_id=1, source_target_pairs={{0,6},{1,7},{2,4},{3,5},{4,2},{5,3},{6,0},{7,1},{8,14},{9,15},{10,... | collective-permute-start | bytes 147464 | tf_op jit(solution)/shard_map/ppermute | solution.py:1188
  176.2 7.7 %collective-permute-start.15 = (bf16[768,128]{1,0:T(8,128)(2,1)S(1)}, bf16[768,128]{1,0:T(8,128)(2,1)S(1)}, u32[]{:S(2)}, u32[]{:S(2)}) collective-permute-start(bf16[768,128]{1,0:T(8,128)(2,1)S(1)} %pad_maximum_fusion.3.refs_0_), channel_id=1, source_target_pairs={{0,1},{1,0},{2,3},{3,2},{4,5},{5,4},{6,7},{7,6},{8,9},{9,8},{10,11... | collective-permute-start | bytes 589832 | tf_op jit(solution)/shard_map/ppermute | solution.py:1188
  177.4 9.4 %collective-permute-start.16 = (bf16[768,128]{1,0:T(8,128)(2,1)S(1)}, bf16[768,128]{1,0:T(8,128)(2,1)S(1)}, u32[]{:S(2)}, u32[]{:S(2)}) collective-permute-start(bf16[768,128]{1,0:T(8,128)(2,1)S(1)} %pad_maximum_fusion.3.refs_0_), channel_id=1, source_target_pairs={{0,16},{1,17},{2,18},{3,19},{4,20},{5,21},{6,22},{7,23},{8,24},{9,... | collective-permute-start | bytes 589832 | tf_op jit(solution)/shard_map/ppermute | solution.py:1188
  178.6 8.7 %collective-permute-start.17 = (bf16[768,128]{1,0:T(8,128)(2,1)S(1)}, bf16[768,128]{1,0:T(8,128)(2,1)S(1)}, u32[]{:S(2)}, u32[]{:S(2)}) collective-permute-start(bf16[768,128]{1,0:T(8,128)(2,1)S(1)} %pad_maximum_fusion.3.refs_0_), channel_id=1, source_target_pairs={{0,17},{1,16},{2,19},{3,18},{4,21},{5,20},{6,23},{7,22},{8,25},{9,... | collective-permute-start | bytes 589832 | tf_op jit(solution)/shard_map/ppermute | solution.py:1188
  179.0 10.7 %collective-permute-start.3 = (bf16[3,80,384]{2,1,0:T(8,128)(2,1)S(1)}, bf16[3,80,384]{2,1,0:T(8,128)(2,1)S(1)}, u32[]{:S(2)}, u32[]{:S(2)}) collective-permute-start(bf16[3,80,384]{2,1,0:T(8,128)(2,1)S(1)} %add_convert_fusion.4), channel_id=1, source_target_pairs={{0,8},{8,0},{16,24},{24,16},{1,9},{9,1},{17,25},{25,17},{2,10},{10... | collective-permute-start | bytes 552968 | tf_op jit(solution)/shard_map/ppermute | solution.py:1170
  183.8 7.6 %collective-permute-start.18 = (bf16[768,128]{1,0:T(8,128)(2,1)S(1)}, bf16[768,128]{1,0:T(8,128)(2,1)S(1)}, u32[]{:S(2)}, u32[]{:S(2)}) collective-permute-start(bf16[768,128]{1,0:T(8,128)(2,1)S(1)} %pad_maximum_fusion.3.refs_0_), channel_id=1, source_target_pairs={{0,8},{8,0},{16,24},{24,16},{1,9},{9,1},{17,25},{25,17},{2,10},{10... | collective-permute-start | bytes 589832 | tf_op jit(solution)/shard_map/ppermute | solution.py:1170
  183.9 7.5 %collective-permute-start.19 = (bf16[768,128]{1,0:T(8,128)(2,1)S(1)}, bf16[768,128]{1,0:T(8,128)(2,1)S(1)}, u32[]{:S(2)}, u32[]{:S(2)}) collective-permute-start(bf16[768,128]{1,0:T(8,128)(2,1)S(1)} %collective-permute-done.15.refs_1_), channel_id=1, source_target_pairs={{0,8},{8,0},{16,24},{24,16},{1,9},{9,1},{17,25},{25,17},{2,10},{10... | collective-permute-start | bytes 589832 | tf_op jit(solution)/shard_map/ppermute | solution.py:1170
  186.9 4.5 %collective-permute-start.20 = (bf16[768,128]{1,0:T(8,128)(2,1)S(1)}, bf16[768,128]{1,0:T(8,128)(2,1)S(1)}, u32[]{:S(2)}, u32[]{:S(2)}) collective-permute-start(bf16[768,128]{1,0:T(8,128)(2,1)S(1)} %collective-permute-done.16.refs_2_), channel_id=1, source_target_pairs={{0,8},{8,0},{16,24},{24,16},{1,9},{9,1},{17,25},{25,17},{2,10},{10... | collective-permute-start | bytes 589832 | tf_op jit(solution)/shard_map/ppermute | solution.py:1170
  187.3 4.1 %collective-permute-start.21 = (bf16[768,128]{1,0:T(8,128)(2,1)S(1)}, bf16[768,128]{1,0:T(8,128)(2,1)S(1)}, u32[]{:S(2)}, u32[]{:S(2)}) collective-permute-start(bf16[768,128]{1,0:T(8,128)(2,1)S(1)} %collective-permute-done.17.refs_3_), channel_id=1, source_target_pairs={{0,8},{8,0},{16,24},{24,16},{1,9},{9,1},{17,25},{25,17},{2,10},{10... | collective-permute-start | bytes 589832 | tf_op jit(solution)/shard_map/ppermute | solution.py:1170
  (15 other events, 100.8 us)

commit v3 on v2

--- a/solution.py
+++ b/solution.py
@@ -675,7 +675,7 @@
                 at = pl.ds(pl.multiple_of(number * 256, 256), 256)
                 kept_at = pl.ds(pl.multiple_of(bit * half + number * 256, 256), 256)
                 sent_at = pl.ds(pl.multiple_of((1 - bit) * half + number * 256, 256), 256)
-                kept_ref[at, :] = acc_s[kept_at, :]
+                kept_ref[at, :] = acc_s[kept_at, :].astype(bf16)
                 sent_ref[at, :] = acc_s[sent_at, :].astype(bf16)
                 return carry
 
@@ -1085,7 +1085,7 @@
         in_specs += [any_space] * 3
         args += handed
         out_specs = [whole((half, PAIR)), whole((half, PAIR)), proj_spec, proj_spec]
-        out_shape = [shape_of((half, PAIR), f32), shape_of((half, PAIR), bf16)] + proj_shapes
+        out_shape = [shape_of((half, PAIR), bf16), shape_of((half, PAIR), bf16)] + proj_shapes
     else:
         out_specs = [proj_spec, proj_spec] + [any_space] * 3
         out_shape = proj_shapes + hand_shapes

time: 198 us -> 200 us (1.010)
  waiting for transfers between devices: 10.8 us -> 12.8 us
  transfers between devices with their start and end apart: 24 -> 24, of which waited for: 6 -> 8; matrix products, arithmetic and copies ran while one was open for 4% -> 4% of each run, Pallas kernels for 36% -> 35%
where the time goes in v3:
time: 200 us; the launch traced here: 199 us
  Pallas kernels  128 us (64%)
  starting transfers between devices  40.8 us (20%)
  waiting for transfers between devices  12.8 us (6%)
  other arithmetic  11.1 us (6%)
  local copies, waits for them, and re-layouts  3.75 us (2%)
    pallas_call x5, Pallas kernels, kernel_call(): pl.pallas_call(kernel, grid_spec=pltpu.PrefetchScalarGridSpec(num_scalar_...  128 us
    ppermute x9, starting transfers between devices, across_core(): return lax.ppermute(value, 'seq', core_pairs)  14.6 us
    all_to_all x2, starting transfers between devices, swap(): return lax.all_to_all(chunks, AXES, 0, 0, axis_index_groups=members)  14.1 us
    ppermute x12, starting transfers between devices, across(): return lax.ppermute(value, AXES, pairs)  11.7 us
    ppermute x12, waiting for transfers between devices, across(): return lax.ppermute(value, AXES, pairs)  6.67 us
    ppermute x9, waiting for transfers between devices, across_core(): return lax.ppermute(value, 'seq', core_pairs)  5.57 us
  transfers between devices with their start and end apart: 24, of which 8 were waited for; matrix products, arithmetic and copies ran while one was open for 4% of the time, Pallas kernels for 35%

profile of v3, /device:TPU:1, one launch (start us, length us, event | category | flops | bytes accessed | tf_op | source)
XLA Modules:
  0.0 199.2 jit_solution(3001721655700299954)
XLA Ops:
  2.5 52.7 %forward.1 = (bf16[1176,384]{1,0:T(8,128)(2,1)}, bf16[1176,128]{1,0:T(8,128)(2,1)}, f32[8,128]{1,0:T(8,128)}, bf16[1176,384]{1,0:T(8,128)(2,1)}, f32[1176,384]{1...) custom-call(s32[3]{0:T(128)} %pad_add_fusion.start_ref, ...), custom_call_target="tpu_custom_call" | custom-call | flops 40000000000 | bytes 60000000 | tf_op jit(solution)/shard_map/forward/pallas_call | solution.py:854
  55.4 3.3 %collective-permute-done = bf16[5376,128]{1,0:T(8,128)(2,1)S(1)} collective-permute-done((bf16[5376,128]{1,0:T(8,128)(2,1)}, bf16[5376,128]{1,0:T(8,128)(2,1)S(1)}, u32[]{:S(2)}, u32[]{:S(2)}) %collective-permute-start) | collective-permute-done | bytes 1376288 | tf_op jit(solution)/shard_map/ppermute | solution.py:1170
  58.7 2.8 %add_convert_fusion = bf16[5376,128]{1,0:T(8,128)(2,1)} fusion(bf16[5376,128]{1,0:T(8,128)(2,1)S(1)} %collective-permute-done, bf16[5376,128]{1,0:T(8,128)(2,1)} %get-tuple-element.76), kind=kLoop, calls=%fused_computation | loop fusion | flops 2752512 | bytes 4128768 | tf_op jit(solution)/shard_map/convert_element_type | solution.py:1262
  61.4 7.7 %all-to-all-start = ((bf16[16,336,128]{2,1,0:T(8,128)(2,1)}), bf16[16,336,128]{2,1,0:T(8,128)(2,1)S(1)}, u32[]{:S(2)}, u32[]{:S(2)}) async-start(bf16[16,336,128]{2,1,0:T(8,128)(2,1)} %bitcast.5), calls=%async_computation | async-start | bytes 2752512 | tf_op jit(solution)/shard_map/all_to_all | solution.py:1174
  69.2 34.3 %backward.2 = (f32[1,80,384]{2,1,0:T(8,128)}, bf16[1,80,384]{2,1,0:T(8,128)(2,1)}, f32[6144,128]{1,0:T(8,128)}, bf16[392,384]{1,0:T(8,128)(2,1)}, bf16[1568,768]{1,0:T(8,128)(2,1)}) custom-call(s32[3]{0:T(128)} %pad_add_fusion.start_ref, bf16[3,392,384]{2,1,0:T(8,128)(2,1)} %get-tuple-element.79.q_ref, bf16[3,1568,384]{2,1,0:T(8,128)(2,1)} %get-tuple-element.80.k_ref, ...), custom_call_target="tpu_custom_call" | custom-call | flops 32000000000 | bytes 40000000 | tf_op jit(solution)/shard_map/backward/pallas_call | solution.py:854
  104.9 6.3 %all-to-all-start.1 = ((bf16[16,336,128]{2,1,0:T(8,128)(2,1)}), bf16[16,336,128]{2,1,0:T(8,128)(2,1)S(1)}, u32[]{:S(2)}, u32[]{:S(2)}) async-start(bf16[16,336,128]{2,1,0:T(8,128)(2,1)} %broadcast_in_dim.10), calls=%async_computation.1 | async-start | bytes 2752512 | tf_op jit(solution)/shard_map/all_to_all | solution.py:1174
  111.3 29.6 %backward.3 = (bf16[3072,128]{1,0:T(8,128)(2,1)}, bf16[3072,128]{1,0:T(8,128)(2,1)}, f32[2,80,384]{2,1,0:T(8,128)}, bf16[2,80,384]{2,1,0:T(8,128)(2,1)}) custom-call(s32[3]{0:T(128)} %pad_add_fusion.start_ref, bf16[3,392,384]{2,1,0:T(8,128)(2,1)} %get-tuple-element.79.q_ref, bf16[3,1568,384]{2,1,0:T(8,128)(2,1)} %get-tuple-element.80.k_ref, ...), custom_call_target="tpu_custom_call" | custom-call | flops 16000000000 | bytes 20000000 | tf_op jit(solution)/shard_map/backward/pallas_call | solution.py:854
  140.9 1.3 collective-permute-start.4
  142.2 2.3 %collective-permute-done.4 = bf16[3072,128]{1,0:T(8,128)(2,1)} collective-permute-done((bf16[3072,128]{1,0:T(8,128)(2,1)}, bf16[3072,128]{1,0:T(8,128)(2,1)}, u32[]{:S(2)}, u32[]{:S(2)}) %collective-permute-start.4) | collective-permute-done | bytes 786464 | tf_op jit(solution)/shard_map/ppermute | solution.py:1170
  145.0 1.8 collective-permute-start.8
  146.7 2.4 %add_convert_fusion.1 = (bf16[768,128]{1,0:T(8,128)(2,1)S(1)}, bf16[768,128]{1,0:T(8,128)(2,1)S(1)}, bf16[768,128]{1,0:T(8,128)(2,1)}, f32[768,128]{1,0:T(8,128)S(1)}) fusion(bf16[3072,128]{1,0:T(8,128)(2,1)} %collective-permute-done.4, s32[]{:T(128)S(6)} %select_n.71, bf16[3072,128]{1,0:T(8,128)(2,1)} %get-tuple-element.100, s32[]{:T(128)S(6)} %select_n.70, ...), kind=kLoop, calls=%fused_computation.3 | loop fusion | flops 1474560 | bytes 2555920 | tf_op jit(solution)/shard_map/convert_element_type | solution.py:1199
  150.1 1.6 collective-permute-start.7
  151.7 1.5 pad_maximum_fusion.4
  153.2 1.3 collective-permute-start.1
  155.7 6.1 %assemble_fc.1 = (f32[384,384]{1,0:T(8,128)}, f32[384,1536]{1,0:T(8,128)}, f32[1536,384]{1,0:T(8,128)}, f32[384]{0:T(512)}, f32[384]{0:T(512)}, /*index=5*/f32[3...) custom-call(s32[3]{0:T(128)} %pad_add_fusion.start_ref, bf16[5376,128]{1,0:T(8,128)(2,1)} %bitcast.11, ...), custom_call_target="tpu_custom_call" | custom-call | flops 10000000 | bytes 8000000 | tf_op jit(solution)/shard_map/assemble_fc/pallas_call | solution.py:854
  168.6 1.6 collective-permute-done.9
  171.5 2.1 %collective-permute-start.13 = (bf16[192,128]{1,0:T(8,128)(2,1)S(1)}, bf16[192,128]{1,0:T(8,128)(2,1)S(1)}, u32[]{:S(2)}, u32[]{:S(2)}) collective-permute-start(bf16[192,128]{1,0:T(8,128)(2,1)S(1)} %add_convert_fusion.5), channel_id=1, source_target_pairs={{0,4},{1,5},{2,6},{3,7},{4,0},{5,1},{6,2},{7,3},{8,12},{9,13},{10,... | collective-permute-start | bytes 147464 | tf_op jit(solution)/shard_map/ppermute | solution.py:1188
  175.4 2.9 %collective-permute-done.14 = bf16[192,128]{1,0:T(8,128)(2,1)S(1)} collective-permute-done((bf16[192,128]{1,0:T(8,128)(2,1)S(1)}, bf16[192,128]{1,0:T(8,128)(2,1)S(1)}, u32[]{:S(2)}, u32[]{:S(2)}) %collective-permute-start.14) | collective-permute-done | bytes 49184 | tf_op jit(solution)/shard_map/ppermute | solution.py:1188
  178.3 1.4 collective-permute-start.15
  181.1 3.1 %collective-permute-start.3 = (bf16[3,80,384]{2,1,0:T(8,128)(2,1)S(1)}, bf16[3,80,384]{2,1,0:T(8,128)(2,1)S(1)}, u32[]{:S(2)}, u32[]{:S(2)}) collective-permute-start(bf16[3,80,384]{2,1,0:T(8,128)(2,1)S(1)} %add_convert_fusion.4), channel_id=1, source_target_pairs={{0,8},{8,0},{16,24},{24,16},{1,9},{9,1},{17,25},{25,17},{2,10},{10... | collective-permute-start | bytes 552968 | tf_op jit(solution)/shard_map/ppermute | solution.py:1170
  184.3 4.1 %collective-permute-start.19 = (bf16[768,128]{1,0:T(8,128)(2,1)S(1)}, bf16[768,128]{1,0:T(8,128)(2,1)S(1)}, u32[]{:S(2)}, u32[]{:S(2)}) collective-permute-start(bf16[768,128]{1,0:T(8,128)(2,1)S(1)} %collective-permute-done.15.refs_1_), channel_id=1, source_target_pairs={{0,8},{8,0},{16,24},{24,16},{1,9},{9,1},{17,25},{25,17},{2,10},{10... | collective-permute-start | bytes 589832 | tf_op jit(solution)/shard_map/ppermute | solution.py:1170
  189.1 2.1 %collective-permute-start.21 = (bf16[768,128]{1,0:T(8,128)(2,1)S(1)}, bf16[768,128]{1,0:T(8,128)(2,1)S(1)}, u32[]{:S(2)}, u32[]{:S(2)}) collective-permute-start(bf16[768,128]{1,0:T(8,128)(2,1)S(1)} %collective-permute-done.17.refs_3_), channel_id=1, source_target_pairs={{0,8},{8,0},{16,24},{24,16},{1,9},{9,1},{17,25},{25,17},{2,10},{10... | collective-permute-start | bytes 589832 | tf_op jit(solution)/shard_map/ppermute | solution.py:1170
  191.2 1.7 fusion
  193.8 5.2 %assemble_qkv.1 = (f32[768,384]{1,0:T(8,128)}, f32[384,1152]{1,0:T(8,128)}, f32[384]{0:T(512)}, f32[384]{0:T(512)}, f32[384]{0:T(512)}, /*index=5*/f32[384]{0:T(...) custom-call(s32[3]{0:T(128)} %pad_add_fusion.start_ref, bf16[768,128]{1,0:T(8,128)(2,1)} %copy-done.2, ...), custom_call_target="tpu_custom_call" | custom-call | flops 10000000 | bytes 5000000 | tf_op jit(solution)/shard_map/assemble_qkv/pallas_call | solution.py:854
  (72 shorter events, 19.0 us)
Async XLA Ops:
  55.2 3.4 %collective-permute-start = (bf16[5376,128]{1,0:T(8,128)(2,1)}, bf16[5376,128]{1,0:T(8,128)(2,1)S(1)}, u32[]{:S(2)}, u32[]{:S(2)}) collective-permute-start(bf16[5376,128]{1,0:T(8,128)(2,1)} %get-tuple-element.77), channel_id=1, source_target_pairs={{0,8},{8,0},{16,24},{24,16},{1,9},{9,1},{17,25},{25,17},{2,10},{10... | collective-permute-start | bytes 4128776 | tf_op jit(solution)/shard_map/ppermute | solution.py:1170
  61.4 42.0 %all-to-all-start = ((bf16[16,336,128]{2,1,0:T(8,128)(2,1)}), bf16[16,336,128]{2,1,0:T(8,128)(2,1)S(1)}, u32[]{:S(2)}, u32[]{:S(2)}) async-start(bf16[16,336,128]{2,1,0:T(8,128)(2,1)} %bitcast.5), calls=%async_computation | async-start | bytes 2752512 | tf_op jit(solution)/shard_map/all_to_all | solution.py:1174
  104.9 40.0 %all-to-all-start.1 = ((bf16[16,336,128]{2,1,0:T(8,128)(2,1)}), bf16[16,336,128]{2,1,0:T(8,128)(2,1)S(1)}, u32[]{:S(2)}, u32[]{:S(2)}) async-start(bf16[16,336,128]{2,1,0:T(8,128)(2,1)} %broadcast_in_dim.10), calls=%async_computation.1 | async-start | bytes 2752512 | tf_op jit(solution)/shard_map/all_to_all | solution.py:1174
  140.9 3.5 %collective-permute-start.4 = (bf16[3072,128]{1,0:T(8,128)(2,1)}, bf16[3072,128]{1,0:T(8,128)(2,1)}, u32[]{:S(2)}, u32[]{:S(2)}) collective-permute-start(bf16[3072,128]{1,0:T(8,128)(2,1)} %get-tuple-element.102), channel_id=1, source_target_pairs={{0,8},{8,0},{16,24},{24,16},{1,9},{9,1},{17,25},{25,17},{2,10},{10... | collective-permute-start | bytes 2359304 | tf_op jit(solution)/shard_map/ppermute | solution.py:1170
  145.0 9.6 %collective-permute-start.8 = (bf16[5376,128]{1,0:T(8,128)(2,1)S(1)}, bf16[5376,128]{1,0:T(8,128)(2,1)S(1)}, u32[]{:S(2)}, u32[]{:S(2)}) collective-permute-start(bf16[5376,128]{1,0:T(8,128)(2,1)S(1)} %bitcast.10), channel_id=1, source_target_pairs={{0,8},{8,0},{16,24},{24,16},{1,9},{9,1},{17,25},{25,17},{2,10},{10... | collective-permute-start | bytes 4128776 | tf_op jit(solution)/shard_map/ppermute | solution.py:1170
  149.1 12.7 %collective-permute-start.5 = (bf16[768,128]{1,0:T(8,128)(2,1)}, bf16[768,128]{1,0:T(8,128)(2,1)}, u32[]{:S(2)}, u32[]{:S(2)}) collective-permute-start(bf16[768,128]{1,0:T(8,128)(2,1)} %get-tuple-element.132), channel_id=1, source_target_pairs={{0,1},{1,0},{2,3},{3,2},{4,5},{5,4},{6,7},{7,6},{8,9},{9,8},{10,11... | collective-permute-start | bytes 589832 | tf_op jit(solution)/shard_map/ppermute | solution.py:1188
  149.1 12.8 %collective-permute-start.6 = (bf16[768,128]{1,0:T(8,128)(2,1)S(1)}, bf16[768,128]{1,0:T(8,128)(2,1)}, u32[]{:S(2)}, u32[]{:S(2)}) collective-permute-start(bf16[768,128]{1,0:T(8,128)(2,1)S(1)} %get-tuple-element.131), channel_id=1, source_target_pairs={{0,16},{1,17},{2,18},{3,19},{4,20},{5,21},{6,22},{7,23},{8,24},{9,... | collective-permute-start | bytes 589832 | tf_op jit(solution)/shard_map/ppermute | solution.py:1188
  150.1 11.7 %collective-permute-start.7 = (bf16[768,128]{1,0:T(8,128)(2,1)S(1)}, bf16[768,128]{1,0:T(8,128)(2,1)}, u32[]{:S(2)}, u32[]{:S(2)}) collective-permute-start(bf16[768,128]{1,0:T(8,128)(2,1)S(1)} %get-tuple-element.130), channel_id=1, source_target_pairs={{0,17},{1,16},{2,19},{3,18},{4,21},{5,20},{6,23},{7,22},{8,25},{9,... | collective-permute-start | bytes 589832 | tf_op jit(solution)/shard_map/ppermute | solution.py:1188
  153.2 12.4 %collective-permute-start.1 = (bf16[3,80,384]{2,1,0:T(8,128)(2,1)}, bf16[3,80,384]{2,1,0:T(8,128)(2,1)}, u32[]{:S(2)}, u32[]{:S(2)}) collective-permute-start(bf16[3,80,384]{2,1,0:T(8,128)(2,1)} %pad_maximum_fusion.4), channel_id=1, source_target_pairs={{0,8},{8,0},{16,24},{24,16},{1,9},{9,1},{17,25},{25,17},{2,10},{10... | collective-permute-start | bytes 552968 | tf_op jit(solution)/shard_map/ppermute | solution.py:1170
  163.0 5.1 %collective-permute-start.10 = (bf16[192,128]{1,0:T(8,128)(2,1)S(1)}, bf16[192,128]{1,0:T(8,128)(2,1)S(1)}, u32[]{:S(2)}, u32[]{:S(2)}) collective-permute-start(bf16[192,128]{1,0:T(8,128)(2,1)S(1)} %get-tuple-element.136), channel_id=1, source_target_pairs={{0,4},{1,5},{2,6},{3,7},{4,0},{5,1},{6,2},{7,3},{8,12},{9,13},{10,... | collective-permute-start | bytes 147464 | tf_op jit(solution)/shard_map/ppermute | solution.py:1188
  163.7 4.9 %collective-permute-start.11 = (bf16[192,128]{1,0:T(8,128)(2,1)S(1)}, bf16[192,128]{1,0:T(8,128)(2,1)S(1)}, u32[]{:S(2)}, u32[]{:S(2)}) collective-permute-start(bf16[192,128]{1,0:T(8,128)(2,1)S(1)} %get-tuple-element.135), channel_id=1, source_target_pairs={{0,6},{1,7},{2,4},{3,5},{4,2},{5,3},{6,0},{7,1},{8,14},{9,15},{10,... | collective-permute-start | bytes 147464 | tf_op jit(solution)/shard_map/ppermute | solution.py:1188
  164.9 5.3 %collective-permute-start.9 = (bf16[192,128]{1,0:T(8,128)(2,1)S(1)}, bf16[192,128]{1,0:T(8,128)(2,1)S(1)}, u32[]{:S(2)}, u32[]{:S(2)}) collective-permute-start(bf16[192,128]{1,0:T(8,128)(2,1)S(1)} %get-tuple-element.134), channel_id=1, source_target_pairs={{0,2},{1,3},{2,0},{3,1},{4,6},{5,7},{6,4},{7,5},{8,10},{9,11},{10,... | collective-permute-start | bytes 147464 | tf_op jit(solution)/shard_map/ppermute | solution.py:1188
  166.7 14.4 %collective-permute-start.2 = (bf16[3,80,384]{2,1,0:T(8,128)(2,1)S(1)}, bf16[3,80,384]{2,1,0:T(8,128)(2,1)S(1)}, u32[]{:S(2)}, u32[]{:S(2)}) collective-permute-start(bf16[3,80,384]{2,1,0:T(8,128)(2,1)S(1)} %fusion.6), channel_id=1, source_target_pairs={{0,16},{8,24},{16,0},{24,8},{1,17},{9,25},{17,1},{25,9},{2,18},{10... | collective-permute-start | bytes 552968 | tf_op jit(solution)/shard_map/ppermute | solution.py:1284
  171.1 3.6 %collective-permute-start.12 = (bf16[192,128]{1,0:T(8,128)(2,1)S(1)}, bf16[192,128]{1,0:T(8,128)(2,1)S(1)}, u32[]{:S(2)}, u32[]{:S(2)}) collective-permute-start(bf16[192,128]{1,0:T(8,128)(2,1)S(1)} %add_convert_fusion.5), channel_id=1, source_target_pairs={{0,2},{1,3},{2,0},{3,1},{4,6},{5,7},{6,4},{7,5},{8,10},{9,11},{10,... | collective-permute-start | bytes 147464 | tf_op jit(solution)/shard_map/ppermute | solution.py:1188
  171.5 3.9 %collective-permute-start.13 = (bf16[192,128]{1,0:T(8,128)(2,1)S(1)}, bf16[192,128]{1,0:T(8,128)(2,1)S(1)}, u32[]{:S(2)}, u32[]{:S(2)}) collective-permute-start(bf16[192,128]{1,0:T(8,128)(2,1)S(1)} %add_convert_fusion.5), channel_id=1, source_target_pairs={{0,4},{1,5},{2,6},{3,7},{4,0},{5,1},{6,2},{7,3},{8,12},{9,13},{10,... | collective-permute-start | bytes 147464 | tf_op jit(solution)/shard_map/ppermute | solution.py:1188
  173.6 4.7 %collective-permute-start.14 = (bf16[192,128]{1,0:T(8,128)(2,1)S(1)}, bf16[192,128]{1,0:T(8,128)(2,1)S(1)}, u32[]{:S(2)}, u32[]{:S(2)}) collective-permute-start(bf16[192,128]{1,0:T(8,128)(2,1)S(1)} %add_convert_fusion.5), channel_id=1, source_target_pairs={{0,6},{1,7},{2,4},{3,5},{4,2},{5,3},{6,0},{7,1},{8,14},{9,15},{10,... | collective-permute-start | bytes 147464 | tf_op jit(solution)/shard_map/ppermute | solution.py:1188
  178.3 6.0 %collective-permute-start.15 = (bf16[768,128]{1,0:T(8,128)(2,1)S(1)}, bf16[768,128]{1,0:T(8,128)(2,1)S(1)}, u32[]{:S(2)}, u32[]{:S(2)}) collective-permute-start(bf16[768,128]{1,0:T(8,128)(2,1)S(1)} %pad_maximum_fusion.3.refs_0_), channel_id=1, source_target_pairs={{0,1},{1,0},{2,3},{3,2},{4,5},{5,4},{6,7},{7,6},{8,9},{9,8},{10,11... | collective-permute-start | bytes 589832 | tf_op jit(solution)/shard_map/ppermute | solution.py:1188
  179.7 8.7 %collective-permute-start.16 = (bf16[768,128]{1,0:T(8,128)(2,1)S(1)}, bf16[768,128]{1,0:T(8,128)(2,1)S(1)}, u32[]{:S(2)}, u32[]{:S(2)}) collective-permute-start(bf16[768,128]{1,0:T(8,128)(2,1)S(1)} %pad_maximum_fusion.3.refs_0_), channel_id=1, source_target_pairs={{0,16},{1,17},{2,18},{3,19},{4,20},{5,21},{6,22},{7,23},{8,24},{9,... | collective-permute-start | bytes 589832 | tf_op jit(solution)/shard_map/ppermute | solution.py:1188
  180.9 8.2 %collective-permute-start.17 = (bf16[768,128]{1,0:T(8,128)(2,1)S(1)}, bf16[768,128]{1,0:T(8,128)(2,1)S(1)}, u32[]{:S(2)}, u32[]{:S(2)}) collective-permute-start(bf16[768,128]{1,0:T(8,128)(2,1)S(1)} %pad_maximum_fusion.3.refs_0_), channel_id=1, source_target_pairs={{0,17},{1,16},{2,19},{3,18},{4,21},{5,20},{6,23},{7,22},{8,25},{9,... | collective-permute-start | bytes 589832 | tf_op jit(solution)/shard_map/ppermute | solution.py:1188
  181.1 10.1 %collective-permute-start.3 = (bf16[3,80,384]{2,1,0:T(8,128)(2,1)S(1)}, bf16[3,80,384]{2,1,0:T(8,128)(2,1)S(1)}, u32[]{:S(2)}, u32[]{:S(2)}) collective-permute-start(bf16[3,80,384]{2,1,0:T(8,128)(2,1)S(1)} %add_convert_fusion.4), channel_id=1, source_target_pairs={{0,8},{8,0},{16,24},{24,16},{1,9},{9,1},{17,25},{25,17},{2,10},{10... | collective-permute-start | bytes 552968 | tf_op jit(solution)/shard_map/ppermute | solution.py:1170
  184.2 8.7 %collective-permute-start.18 = (bf16[768,128]{1,0:T(8,128)(2,1)S(1)}, bf16[768,128]{1,0:T(8,128)(2,1)S(1)}, u32[]{:S(2)}, u32[]{:S(2)}) collective-permute-start(bf16[768,128]{1,0:T(8,128)(2,1)S(1)} %pad_maximum_fusion.3.refs_0_), channel_id=1, source_target_pairs={{0,8},{8,0},{16,24},{24,16},{1,9},{9,1},{17,25},{25,17},{2,10},{10... | collective-permute-start | bytes 589832 | tf_op jit(solution)/shard_map/ppermute | solution.py:1170
  184.3 8.6 %collective-permute-start.19 = (bf16[768,128]{1,0:T(8,128)(2,1)S(1)}, bf16[768,128]{1,0:T(8,128)(2,1)S(1)}, u32[]{:S(2)}, u32[]{:S(2)}) collective-permute-start(bf16[768,128]{1,0:T(8,128)(2,1)S(1)} %collective-permute-done.15.refs_1_), channel_id=1, source_target_pairs={{0,8},{8,0},{16,24},{24,16},{1,9},{9,1},{17,25},{25,17},{2,10},{10... | collective-permute-start | bytes 589832 | tf_op jit(solution)/shard_map/ppermute | solution.py:1170
  188.4 4.6 %collective-permute-start.20 = (bf16[768,128]{1,0:T(8,128)(2,1)S(1)}, bf16[768,128]{1,0:T(8,128)(2,1)S(1)}, u32[]{:S(2)}, u32[]{:S(2)}) collective-permute-start(bf16[768,128]{1,0:T(8,128)(2,1)S(1)} %collective-permute-done.16.refs_2_), channel_id=1, source_target_pairs={{0,8},{8,0},{16,24},{24,16},{1,9},{9,1},{17,25},{25,17},{2,10},{10... | collective-permute-start | bytes 589832 | tf_op jit(solution)/shard_map/ppermute | solution.py:1170
  189.1 3.8 %collective-permute-start.21 = (bf16[768,128]{1,0:T(8,128)(2,1)S(1)}, bf16[768,128]{1,0:T(8,128)(2,1)S(1)}, u32[]{:S(2)}, u32[]{:S(2)}) collective-permute-start(bf16[768,128]{1,0:T(8,128)(2,1)S(1)} %collective-permute-done.17.refs_3_), channel_id=1, source_target_pairs={{0,8},{8,0},{16,24},{24,16},{1,9},{9,1},{17,25},{25,17},{2,10},{10... | collective-permute-start | bytes 589832 | tf_op jit(solution)/shard_map/ppermute | solution.py:1170
  (14 other events, 102.2 us)
